TPU v7x, 32 devices: a whole 2x2x4 slice. The times are simulated.
32 devices in a mesh: dp: 4 (over y, x), seq: 4 (over z), head: 2 (over core).
Axes of the slice: x: 2, y: 2, z: 4, core: 2. Of those that a mesh axis runs over, the one named last changes fastest.
Arguments:
- hidden_in: bfloat16 [4, 512, 1024], P('dp', 'seq'), may hold values from -10 to 10
- out_grad: bfloat16 [4, 512, 1024], P('dp', 'seq'), may hold values from -6 to 6
- doc_ids: int32 [4, 512], P('dp'), may hold values from 0 to 3, never falling along the last dimension, each value on 1 to 256 neighbouring positions
- mixer_gain: bfloat16 [1024], P(('dp', 'seq')), may hold values from 0.5 to 1.5
- ssm_gate_proj: bfloat16 [1024, 1536], P(('dp', 'seq'), 'head'), may hold values from -0.1875 to 0.1875
- ssm_value_proj: bfloat16 [1024, 1536], P(('dp', 'seq'), 'head'), may hold values from -0.1875 to 0.1875
- ssm_bc_proj: bfloat16 [1024, 256], P(('dp', 'seq')), may hold values from -0.1875 to 0.1875
- ssm_step_proj: bfloat16 [1024, 24], P(('dp', 'seq'), 'head'), may hold values from -0.1875 to 0.1875
- conv_value_kernel: float32 [4, 1536], P(None, 'head'), may hold values from -3 to 3
- conv_value_bias: float32 [1536], P('head'), may hold values from -3 to 3
- conv_bc_kernel: float32 [4, 256], replicated, may hold values from -3 to 3
- conv_bc_bias: float32 [256], replicated, may hold values from -3 to 3
- decay_log: float32 [24], P('head'), may hold values from -13 to -3
- step_bias: float32 [24], P('head'), may hold values from -0.5 to 1
- skip_gain: float32 [24], P('head'), may hold values from 0.5 to 1.5
- ssm_norm_gain: float32 [1536], P('head'), may hold values from 0.5 to 1.5
- ssm_out_proj: bfloat16 [1536, 1024], P('head', ('dp', 'seq')), may hold values from -0.15625 to 0.15625
- query_proj: bfloat16 [1024, 512], P(('dp', 'seq'), 'head'), may hold values from -1 to 1
- key_proj: bfloat16 [1024, 128], P(('dp', 'seq'), 'head'), may hold values from -1 to 1
- value_proj: bfloat16 [1024, 128], P(('dp', 'seq'), 'head'), may hold values from -0.1875 to 0.1875
- attn_out_proj: bfloat16 [512, 1024], P('head', ('dp', 'seq')), may hold values from -1.5 to 1.5
- ffn_gain: bfloat16 [1024], P(('dp', 'seq')), may hold values from 0.5 to 1.5
- ffn_gate_proj: bfloat16 [1024, 2048], P(('dp', 'seq'), 'head'), may hold values from -0.1875 to 0.1875
- ffn_up_proj: bfloat16 [1024, 2048], P(('dp', 'seq'), 'head'), may hold values from -0.1875 to 0.1875
- ffn_down_proj: bfloat16 [2048, 1024], P('head', ('dp', 'seq')), may hold values from -0.125 to 0.125
Outputs:
- block_out: bfloat16 [4, 512, 1024], P('dp', 'seq')
- hidden_grad: float32 [4, 512, 1024], P('dp', 'seq')
- grad_mixer_gain: float32 [1024], P(('dp', 'seq'))
- grad_ssm_gate_proj: float32 [1024, 1536], P(('dp', 'seq'), 'head')
- grad_ssm_value_proj: float32 [1024, 1536], P(('dp', 'seq'), 'head')
- grad_ssm_bc_proj: float32 [1024, 256], P(('dp', 'seq'))
- grad_ssm_step_proj: float32 [1024, 24], P(('dp', 'seq'), 'head')
- grad_conv_value_kernel: float32 [4, 1536], P(None, 'head')
- grad_conv_value_bias: float32 [1536], P('head')
- grad_conv_bc_kernel: float32 [4, 256], replicated
- grad_conv_bc_bias: float32 [256], replicated
- grad_decay_log: float32 [24], P('head')
- grad_step_bias: float32 [24], P('head')
- grad_skip_gain: float32 [24], P('head')
- grad_ssm_norm_gain: float32 [1536], P('head')
- grad_ssm_out_proj: float32 [1536, 1024], P('head', ('dp', 'seq'))
- grad_query_proj: float32 [1024, 512], P(('dp', 'seq'), 'head')
- grad_key_proj: float32 [1024, 128], P(('dp', 'seq'), 'head')
- grad_value_proj: float32 [1024, 128], P(('dp', 'seq'), 'head')
- grad_attn_out_proj: float32 [512, 1024], P('head', ('dp', 'seq'))
- grad_ffn_gain: float32 [1024], P(('dp', 'seq'))
- grad_ffn_gate_proj: float32 [1024, 2048], P(('dp', 'seq'), 'head')
- grad_ffn_up_proj: float32 [1024, 2048], P(('dp', 'seq'), 'head')
- grad_ffn_down_proj: float32 [2048, 1024], P('head', ('dp', 'seq'))
Inputs may be any that keep to these rules, and one draw needn't show every extreme that they name: `doc_ids`: along each sequence the ids never fall; one document holds at most 256 tokens, and some document holds exactly that many.
All inputs are finite; a program needn't handle non-finite values.
Results may differ from a plain program's by a relative error of at most 0.028.
Values may be sent and summed in bfloat16 or wider, within the bound.
No kernel may reach another device: no remote copies, remote signals or barrier semaphores. Data moves between devices by JAX's collectives and lax.ppermute only.
A program may use at most 128 MiB of HBM per device.

v0:
```python
from functools import partial

import jax
import jax.numpy as jnp
from jax import lax
from jax.sharding import PartitionSpec as P

HDIM = 64


EPS = 1e-05
HIGH = lax.Precision.HIGHEST
ROPE_BASE = 10000.0
NEG_LARGE = -1e30


def passed_along(block, axis, distance):
    devices = range(lax.axis_size(axis))
    route = [(i - distance, i) for i in devices if i - distance in devices]
    return lax.ppermute(block, axis, route)


def prefix_2(value, axis, join, neutral, backward):
    count, mine = (lax.axis_size(axis), lax.axis_index(axis))
    pieces = jax.tree.map(lambda part: lax.all_gather(part, axis), value)
    if backward:
        pieces = jax.tree.map(lambda part: part[::-1], pieces)
        mine = count - 1 - mine
    total = jax.tree.map(
        lambda part, zero: jnp.full_like(part, 0) + jnp.asarray(zero, part.dtype), value, neutral
    )

    def turn(position, total):
        longer = join(total, jax.tree.map(lambda part: part[position], pieces))
        return jax.tree.map(lambda new, old: jnp.where(position < mine, new, old), longer, total)

    return lax.fori_loop(0, count - 1, turn, total)


def matmul(left, right):
    return jnp.dot(left, right, preferred_element_type=jnp.float32)


def back_product(gradient_term, weight):
    return jnp.einsum("slo,io->sli", gradient_term, weight, preferred_element_type=jnp.float32)


def weight_grad(activation_list, gradient_term):
    return jnp.einsum(
        "yux,yup->xp", activation_list, gradient_term, preferred_element_type=jnp.float32
    )


def rms_apply(values, gain):
    scale = lax.rsqrt(jnp.mean(values * values, axis=-1, keepdims=True) + EPS)
    normed = values * scale
    return (normed, scale, normed * gain.astype(jnp.float32))


def rms_backward(grad_out, normed, scale, gain):
    grad_normed = grad_out * gain.astype(jnp.float32)
    inner = jnp.mean(grad_normed * normed, axis=-1, keepdims=True)
    leading = tuple(range(grad_out.ndim - 1))
    return (scale * (grad_normed - normed * inner), jnp.sum(grad_out * normed, axis=leading))


def rope_tables(positions, width):
    half = width // 2
    frequency = ROPE_BASE ** (-2.0 * jnp.arange(half, dtype=jnp.float32) / width)
    angles = positions.astype(jnp.float32)[:, None] * frequency[None, :]
    return (jnp.cos(angles), jnp.sin(angles))


def rotate(values, cosine, sine, sign):
    half = values.shape[-1] // 2
    first = values[..., :half]
    second = values[..., half:]
    return jnp.concatenate(
        [first * cosine - sign * second * sine, second * cosine + sign * first * sine], axis=-1
    )


def doc_masks(doc_window, width):
    length = doc_window.shape[1] - width
    own = doc_window[:, width:]
    conv_mask = jnp.stack(
        [doc_window[:, offset : offset + length] == own for offset in range(width + 1)], axis=-1
    ).astype(jnp.float32)
    before = doc_window[:, width - 1]
    order = jnp.arange(length, dtype=jnp.int32)
    causal = order[:, None] >= order[None, :]
    same_doc = (own[:, :, None] == own[:, None, :]) & causal[None]
    live = (own == before[:, None]).astype(jnp.float32)
    tail = (own == own[:, length - 1 :]).astype(jnp.float32)
    return (conv_mask, same_doc, live, tail, live[:, length - 1])


def conv_silu(padded, kernel, bias, conv_mask):
    length = conv_mask.shape[1]
    total = bias
    for offset in range(kernel.shape[0]):
        total = (
            total
            + kernel[offset]
            * padded[:, offset : offset + length]
            * conv_mask[:, :, offset : offset + 1]
        )
    return jax.nn.silu(total)


def value_inputs(value_ext, step_raw, kernel, bias, decay_log, step_bias, conv_mask):
    act_value = conv_silu(value_ext, kernel, bias, conv_mask)
    step = jax.nn.softplus(step_raw + step_bias)
    log_decay = -step * jnp.exp(decay_log)
    return (act_value, step, log_decay)


def span_ends(act_value, act_bc, step, log_decay, tail, last_live):
    batch, length, heads = step.shape
    hdim = act_value.shape[-1] // heads
    nstate = act_bc.shape[-1] // 2
    values = act_value.reshape(batch, length, heads, hdim)
    cumul = jnp.cumsum(log_decay, axis=1)
    total = cumul[:, -1]
    weights = jnp.exp(total[:, None, :] - cumul) * step * tail[..., None]
    ends = jnp.einsum("slh,slhp,sln->shpn", weights, values, act_bc[..., :nstate], precision=HIGH)
    return (ends, jnp.exp(total) * last_live[:, None])


def span_gated(act_value, act_bc, step, log_decay, gate_raw, state_in, skip_gain, same_doc, live):
    batch, length, heads = step.shape
    hdim = act_value.shape[-1] // heads
    nstate = act_bc.shape[-1] // 2
    values = act_value.reshape(batch, length, heads, hdim)
    inputs_b = act_bc[..., :nstate]
    readout = act_bc[..., nstate:]
    cumul = jnp.cumsum(log_decay, axis=1)
    within = same_doc[..., None]
    gap = jnp.where(within, cumul[:, :, None, :] - cumul[:, None, :, :], 0.0)
    kernel = jnp.where(within, jnp.exp(gap), 0.0)
    intersection = jnp.einsum("stn,srn->str", readout, inputs_b, precision=HIGH)
    mixing = kernel * intersection[..., None] * step[:, None, :, :]
    intra = jnp.einsum("strh,srhp->sthp", mixing, values, precision=HIGH)
    carried = (
        jnp.einsum("shpn,stn->sthp", state_in, readout, precision=HIGH)
        * (jnp.exp(cumul) * live[..., None])[..., None]
    )
    output = intra + carried + skip_gain[None, None, :, None] * values
    return output.reshape(batch, length, heads * hdim) * jax.nn.silu(gate_raw)


def combine_states(earlier, later):
    return (earlier[0] * later[0], earlier[1] * later[0][:, :, None, None] + later[1])


def head_sum(values):
    return lax.psum(values, "head")


def norm_share(values):
    return lax.psum(values, "head")


def key_block():
    return 512


def block_scores(query_group, key_value_rows, block_start, block, doc_ids, query_pos, query_doc):
    batch, length, key_heads, group, hdim = query_group.shape
    piece = lax.dynamic_slice_in_dim(key_value_rows, block_start, block, 1)
    split = key_heads * hdim
    keys = piece[..., :split].reshape(batch, block, key_heads, hdim)
    values = piece[..., split:].reshape(batch, block, key_heads, hdim)
    scores = jnp.einsum(
        "sqcgd,skcd->scgqk", query_group, keys, preferred_element_type=jnp.float32
    ) * hdim ** (-0.5)
    key_pos = block_start + jnp.arange(block, dtype=jnp.int32)
    key_doc = lax.dynamic_slice_in_dim(doc_ids, block_start, block, 1)
    allowed = (key_pos[None, None, :] <= query_pos[None, :, None]) & (
        key_doc[:, None, :] == query_doc[:, :, None]
    )
    return (scores, allowed[:, None, None], keys, values)


def local(
    hidden_in,
    out_grad,
    doc_ids,
    mixer_gain,
    ssm_gate_proj,
    ssm_value_proj,
    ssm_bc_proj,
    ssm_step_proj,
    conv_value_kernel,
    conv_value_bias,
    conv_bc_kernel,
    conv_bc_bias,
    decay_log,
    step_bias,
    skip_gain,
    ssm_norm_gain,
    ssm_out_proj,
    query_proj,
    key_proj,
    value_proj,
    attn_out_proj,
    ffn_gain,
    ffn_gate_proj,
    ffn_up_proj,
    ffn_down_proj,
):
    batch, length, width = hidden_in.shape
    fetched = (
        lax.all_gather(mixer_gain, ("dp", "seq"), axis=0, tiled=True),
        lax.all_gather(ssm_gate_proj, ("dp", "seq"), axis=0, tiled=True),
        lax.all_gather(ssm_value_proj, ("dp", "seq"), axis=0, tiled=True),
        lax.all_gather(ssm_bc_proj, ("dp", "seq"), axis=0, tiled=True),
        lax.all_gather(ssm_step_proj, ("dp", "seq"), axis=0, tiled=True),
        lax.all_gather(query_proj, ("dp", "seq"), axis=0, tiled=True),
        lax.all_gather(key_proj, ("dp", "seq"), axis=0, tiled=True),
        lax.all_gather(value_proj, ("dp", "seq"), axis=0, tiled=True),
        lax.all_gather(ffn_gain, ("dp", "seq"), axis=0, tiled=True),
        lax.all_gather(ffn_gate_proj, ("dp", "seq"), axis=0, tiled=True),
        lax.all_gather(ffn_up_proj, ("dp", "seq"), axis=0, tiled=True),
        lax.all_gather(ssm_out_proj, ("dp", "seq"), axis=1, tiled=True),
        lax.all_gather(attn_out_proj, ("dp", "seq"), axis=1, tiled=True),
        lax.all_gather(ffn_down_proj, ("dp", "seq"), axis=1, tiled=True),
    )
    (
        full_mixer_gain,
        full_gate_proj,
        full_value_proj,
        full_bc_proj,
        full_step_proj,
        full_query_proj,
        full_key_proj,
        full_attn_value,
        full_ffn_gain,
        full_ffn_gate,
        full_ffn_up,
        full_ssm_out,
        full_attn_out,
        full_ffn_down,
    ) = fetched
    start = lax.axis_index("seq") * length
    conv_width = conv_value_kernel.shape[0] - 1
    query_heads = full_query_proj.shape[1] // HDIM
    key_heads = full_key_proj.shape[1] // HDIM
    group = query_heads // key_heads
    resid = hidden_in.astype(jnp.float32)
    normed_pre, scale_pre, scaled_pre = rms_apply(resid, full_mixer_gain)
    mixer_in = scaled_pre.astype(jnp.bfloat16)
    gate_raw = matmul(mixer_in, full_gate_proj)
    value_raw = matmul(mixer_in, full_value_proj)
    bc_raw = matmul(mixer_in, full_bc_proj)
    step_raw = matmul(mixer_in, full_step_proj)
    doc_pad = jnp.concatenate([jnp.full((batch, conv_width), -1, jnp.int32), doc_ids], axis=1)
    doc_window = lax.dynamic_slice_in_dim(doc_pad, start, length + conv_width, 1)
    conv_mask, same_doc, live, tail, last_live = doc_masks(doc_window, conv_width)
    edges = passed_along(
        (value_raw[:, length - conv_width :], bc_raw[:, length - conv_width :]), "seq", 1
    )
    value_ext = jnp.concatenate([edges[0], value_raw], axis=1)
    bc_ext = jnp.concatenate([edges[1], bc_raw], axis=1)
    (act_value, step, log_decay), value_pull = jax.vjp(
        partial(value_inputs, conv_mask=conv_mask),
        value_ext,
        step_raw,
        conv_value_kernel,
        conv_value_bias,
        decay_log,
        step_bias,
    )
    act_bc, bc_pull = jax.vjp(
        partial(conv_silu, conv_mask=conv_mask), bc_ext, conv_bc_kernel, conv_bc_bias
    )
    (ends, decay), ends_pull = jax.vjp(
        partial(span_ends, tail=tail, last_live=last_live), act_value, act_bc, step, log_decay
    )
    prefix = prefix_2(
        (decay, ends), "seq", combine_states, (jnp.ones_like(decay), jnp.zeros_like(ends)), False
    )
    state_in = prefix[1]
    gated, gated_pull = jax.vjp(
        partial(span_gated, same_doc=same_doc, live=live),
        act_value,
        act_bc,
        step,
        log_decay,
        gate_raw,
        state_in,
        skip_gain,
    )
    inner_width = gated.shape[-1] * lax.axis_size("head")
    square_sum = norm_share(jnp.sum(gated * gated, axis=-1))
    norm_scale = lax.rsqrt(square_sum[..., None] / inner_width + EPS)
    gated_normed = gated * norm_scale
    ssm_in = (gated_normed * ssm_norm_gain).astype(jnp.bfloat16)
    positions = start + jnp.arange(length, dtype=jnp.int32)
    cosine, sine = rope_tables(positions, HDIM)
    cosine = cosine[None, :, None, :]
    sine = sine[None, :, None, :]
    query = rotate(
        matmul(mixer_in, full_query_proj).reshape(batch, length, query_heads, HDIM),
        cosine,
        sine,
        1.0,
    ).astype(jnp.bfloat16)
    keys_new = rotate(
        matmul(mixer_in, full_key_proj).reshape(batch, length, key_heads, HDIM), cosine, sine, 1.0
    ).astype(jnp.bfloat16)
    values_new = matmul(mixer_in, full_attn_value).astype(jnp.bfloat16)
    kv_local = jnp.concatenate(
        [keys_new.reshape(batch, length, key_heads * HDIM), values_new], axis=-1
    )
    key_value_rows = lax.all_gather(kv_local, "seq", axis=1, tiled=True)
    query_group = query.reshape(batch, length, key_heads, group, HDIM)
    query_doc = lax.dynamic_slice_in_dim(doc_ids, start, length, 1)
    block = key_block()
    block_count = (start + length - 1) // block + 1

    def stats_step(index, carry):
        peak, total = carry
        scores, allowed, _, _ = block_scores(
            query_group, key_value_rows, index * block, block, doc_ids, positions, query_doc
        )
        masked = jnp.where(allowed, scores, NEG_LARGE)
        new_peak = jnp.maximum(peak, jnp.max(masked, axis=-1))
        total = total * jnp.exp(peak - new_peak) + jnp.sum(
            jnp.where(allowed, jnp.exp(masked - new_peak[..., None]), 0.0), axis=-1
        )
        return (new_peak, total)

    stat_shape = (batch, key_heads, group, length)
    peak, total = lax.fori_loop(
        0,
        block_count,
        stats_step,
        (jnp.full(stat_shape, NEG_LARGE, jnp.float32), jnp.zeros(stat_shape, jnp.float32)),
    )
    log_total = peak + jnp.log(total)

    def value_step(index, accum):
        scores, allowed, _, values = block_scores(
            query_group, key_value_rows, index * block, block, doc_ids, positions, query_doc
        )
        probs = jnp.where(allowed, jnp.exp(scores - log_total[..., None]), 0.0).astype(jnp.bfloat16)
        return accum + jnp.einsum(
            "scgqk,skcd->sqcgd", probs, values, preferred_element_type=jnp.float32
        )

    attn_out = lax.fori_loop(0, block_count, value_step, jnp.zeros(query_group.shape, jnp.float32))
    attn_in = attn_out.reshape(batch, length, query_heads * HDIM).astype(jnp.bfloat16)
    mixed = resid + head_sum(matmul(ssm_in, full_ssm_out) + matmul(attn_in, full_attn_out))
    normed_ffn, scale_ffn, scaled_ffn = rms_apply(mixed, full_ffn_gain)
    feedforward_input = scaled_ffn.astype(jnp.bfloat16)
    gate = matmul(feedforward_input, full_ffn_gate)
    upward = matmul(feedforward_input, full_ffn_up)
    sigma = jax.nn.sigmoid(gate)
    hidden_act = (gate * sigma * upward).astype(jnp.bfloat16)
    block_out = (mixed + head_sum(matmul(hidden_act, full_ffn_down))).astype(jnp.bfloat16)
    fetched = (
        lax.all_gather(mixer_gain, ("dp", "seq"), axis=0, tiled=True),
        lax.all_gather(ssm_gate_proj, ("dp", "seq"), axis=0, tiled=True),
        lax.all_gather(ssm_value_proj, ("dp", "seq"), axis=0, tiled=True),
        lax.all_gather(ssm_bc_proj, ("dp", "seq"), axis=0, tiled=True),
        lax.all_gather(ssm_step_proj, ("dp", "seq"), axis=0, tiled=True),
        lax.all_gather(query_proj, ("dp", "seq"), axis=0, tiled=True),
        lax.all_gather(key_proj, ("dp", "seq"), axis=0, tiled=True),
        lax.all_gather(value_proj, ("dp", "seq"), axis=0, tiled=True),
        lax.all_gather(ffn_gain, ("dp", "seq"), axis=0, tiled=True),
        lax.all_gather(ffn_gate_proj, ("dp", "seq"), axis=0, tiled=True),
        lax.all_gather(ffn_up_proj, ("dp", "seq"), axis=0, tiled=True),
        lax.all_gather(ssm_out_proj, ("dp", "seq"), axis=1, tiled=True),
        lax.all_gather(attn_out_proj, ("dp", "seq"), axis=1, tiled=True),
        lax.all_gather(ffn_down_proj, ("dp", "seq"), axis=1, tiled=True),
    )
    (
        full_mixer_gain,
        full_gate_proj,
        full_value_proj,
        full_bc_proj,
        full_step_proj,
        full_query_proj,
        full_key_proj,
        full_attn_value,
        full_ffn_gain,
        full_ffn_gate,
        full_ffn_up,
        full_ssm_out,
        full_attn_out,
        full_ffn_down,
    ) = fetched
    grad_top = out_grad.astype(jnp.float32)
    grad_ffn_down = weight_grad(hidden_act, out_grad)
    grad_hidden = back_product(out_grad, full_ffn_down)
    grad_gate_pre = (grad_hidden * upward * sigma * (1.0 + gate * (1.0 - sigma))).astype(
        jnp.bfloat16
    )
    grad_up_pre = (grad_hidden * gate * sigma).astype(jnp.bfloat16)
    grad_ffn_gate = weight_grad(feedforward_input, grad_gate_pre)
    grad_ffn_up = weight_grad(feedforward_input, grad_up_pre)
    grad_ffn_in = head_sum(
        back_product(grad_gate_pre, full_ffn_gate) + back_product(grad_up_pre, full_ffn_up)
    )
    grad_mixed_norm, grad_ffn_gain = rms_backward(grad_ffn_in, normed_ffn, scale_ffn, full_ffn_gain)
    grad_mixed = grad_top + grad_mixed_norm
    branch_gradient = grad_mixed.astype(jnp.bfloat16)
    grad_ssm_out = weight_grad(ssm_in, branch_gradient)
    grad_attn_out = weight_grad(attn_in, branch_gradient)
    grad_ssm = back_product(branch_gradient, full_ssm_out)
    grad_attn = back_product(branch_gradient, full_attn_out).reshape(
        batch, length, key_heads, group, HDIM
    )
    delta = jnp.transpose(jnp.sum(grad_attn * attn_out, axis=-1), (0, 2, 3, 1))
    grad_round = grad_attn.astype(jnp.bfloat16)

    def back_step(index, carry):
        grad_query, grad_kv = carry
        block_start = index * block
        scores, allowed, keys, values = block_scores(
            query_group, key_value_rows, block_start, block, doc_ids, positions, query_doc
        )
        probs = jnp.where(allowed, jnp.exp(scores - log_total[..., None]), 0.0)
        grad_values = jnp.einsum(
            "scgqk,sqcgd->skcd",
            probs.astype(jnp.bfloat16),
            grad_round,
            preferred_element_type=jnp.float32,
        )
        grad_probs = jnp.einsum(
            "sqcgd,skcd->scgqk", grad_round, values, preferred_element_type=jnp.float32
        )
        score_gradients = (probs * (grad_probs - delta[..., None]) * HDIM ** (-0.5)).astype(
            jnp.bfloat16
        )
        grad_query = grad_query + jnp.einsum(
            "scgqk,skcd->sqcgd", score_gradients, keys, preferred_element_type=jnp.float32
        )
        grad_keys = jnp.einsum(
            "scgqk,sqcgd->skcd", score_gradients, query_group, preferred_element_type=jnp.float32
        )
        piece = jnp.concatenate(
            [
                grad_keys.reshape(batch, block, key_heads * HDIM),
                grad_values.reshape(batch, block, key_heads * HDIM),
            ],
            axis=-1,
        )
        return (grad_query, lax.dynamic_update_slice_in_dim(grad_kv, piece, block_start, 1))

    grad_query, grad_kv = lax.fori_loop(
        0,
        block_count,
        back_step,
        (jnp.zeros(query_group.shape, jnp.float32), jnp.zeros(key_value_rows.shape, jnp.float32)),
    )
    grad_kv_own = lax.psum_scatter(grad_kv, "seq", scatter_dimension=1, tiled=True)
    grad_query_in = (
        rotate(grad_query.reshape(batch, length, query_heads, HDIM), cosine, sine, -1.0)
        .reshape(batch, length, query_heads * HDIM)
        .astype(jnp.bfloat16)
    )
    grad_key_in = (
        rotate(
            grad_kv_own[..., : key_heads * HDIM].reshape(batch, length, key_heads, HDIM),
            cosine,
            sine,
            -1.0,
        )
        .reshape(batch, length, key_heads * HDIM)
        .astype(jnp.bfloat16)
    )
    grad_value_in = grad_kv_own[..., key_heads * HDIM :].astype(jnp.bfloat16)
    grad_norm_gain = jnp.sum(grad_ssm * gated_normed, axis=(0, 1))
    scaled_grad = grad_ssm * ssm_norm_gain
    inner = norm_share(jnp.sum(scaled_grad * gated_normed, axis=-1))
    grad_gated = norm_scale * (scaled_grad - gated_normed * (inner[..., None] / inner_width))
    (
        grad_act_value,
        grad_act_bc,
        grad_step,
        grad_log_decay,
        grad_gate_raw,
        grad_state_in,
        grad_skip,
    ) = gated_pull(grad_gated)
    suffix = prefix_2(
        (decay, grad_state_in),
        "seq",
        combine_states,
        (jnp.ones_like(decay), jnp.zeros_like(grad_state_in)),
        True,
    )
    grad_ends = suffix[1]
    grad_decay = jnp.sum(grad_ends * state_in, axis=(2, 3))
    extra_value, extra_bc, extra_step, extra_log = ends_pull((grad_ends, grad_decay))
    (
        grad_value_ext,
        grad_step_raw,
        grad_kernel_value,
        grad_bias_value,
        grad_decay_log,
        grad_step_bias,
    ) = value_pull(
        (grad_act_value + extra_value, grad_step + extra_step, grad_log_decay + extra_log)
    )
    grad_bc_ext, grad_kernel_bc, grad_bias_bc = bc_pull(head_sum(grad_act_bc + extra_bc))
    boundary_gradients = passed_along(
        (grad_value_ext[:, :conv_width], grad_bc_ext[:, :conv_width]), "seq", -1
    )
    grad_value_raw = (
        grad_value_ext[:, conv_width:].at[:, length - conv_width :].add(boundary_gradients[0])
    )
    grad_bc_raw = (
        grad_bc_ext[:, conv_width:].at[:, length - conv_width :].add(boundary_gradients[1])
    )
    grad_gate_in = grad_gate_raw.astype(jnp.bfloat16)
    grad_value_ssm = grad_value_raw.astype(jnp.bfloat16)
    grad_bc_in = grad_bc_raw.astype(jnp.bfloat16)
    grad_step_in = grad_step_raw.astype(jnp.bfloat16)
    partial_sum = (
        back_product(grad_gate_in, full_gate_proj)
        + back_product(grad_value_ssm, full_value_proj)
        + back_product(grad_step_in, full_step_proj)
        + back_product(grad_query_in, full_query_proj)
        + back_product(grad_key_in, full_key_proj)
        + back_product(grad_value_in, full_attn_value)
    )
    grad_mixer_in = head_sum(partial_sum) + back_product(grad_bc_in, full_bc_proj)
    grad_pre_norm, grad_mixer_gain = rms_backward(
        grad_mixer_in, normed_pre, scale_pre, full_mixer_gain
    )
    hidden_grad = grad_mixed + grad_pre_norm
    reduced = (
        lax.psum_scatter(grad_mixer_gain, ("dp", "seq"), scatter_dimension=0, tiled=True),
        lax.psum_scatter(
            weight_grad(mixer_in, grad_gate_in), ("dp", "seq"), scatter_dimension=0, tiled=True
        ),
        lax.psum_scatter(
            weight_grad(mixer_in, grad_value_ssm), ("dp", "seq"), scatter_dimension=0, tiled=True
        ),
        lax.psum_scatter(
            weight_grad(mixer_in, grad_bc_in), ("dp", "seq"), scatter_dimension=0, tiled=True
        ),
        lax.psum_scatter(
            weight_grad(mixer_in, grad_step_in), ("dp", "seq"), scatter_dimension=0, tiled=True
        ),
        lax.psum_scatter(
            weight_grad(mixer_in, grad_query_in), ("dp", "seq"), scatter_dimension=0, tiled=True
        ),
        lax.psum_scatter(
            weight_grad(mixer_in, grad_key_in), ("dp", "seq"), scatter_dimension=0, tiled=True
        ),
        lax.psum_scatter(
            weight_grad(mixer_in, grad_value_in), ("dp", "seq"), scatter_dimension=0, tiled=True
        ),
        lax.psum_scatter(grad_ffn_gain, ("dp", "seq"), scatter_dimension=0, tiled=True),
        lax.psum_scatter(grad_ffn_gate, ("dp", "seq"), scatter_dimension=0, tiled=True),
        lax.psum_scatter(grad_ffn_up, ("dp", "seq"), scatter_dimension=0, tiled=True),
        lax.psum_scatter(grad_ssm_out, ("dp", "seq"), scatter_dimension=1, tiled=True),
        lax.psum_scatter(grad_attn_out, ("dp", "seq"), scatter_dimension=1, tiled=True),
        lax.psum_scatter(grad_ffn_down, ("dp", "seq"), scatter_dimension=1, tiled=True),
    )
    small = lax.psum(
        (
            grad_kernel_value,
            grad_bias_value,
            grad_kernel_bc,
            grad_bias_bc,
            grad_decay_log,
            grad_step_bias,
            grad_skip,
            grad_norm_gain,
        ),
        ("dp", "seq"),
    )
    return (
        block_out,
        hidden_grad,
        reduced[0],
        reduced[1],
        reduced[2],
        reduced[3],
        reduced[4],
        small[0],
        small[1],
        small[2],
        small[3],
        small[4],
        small[5],
        small[6],
        small[7],
        reduced[11],
        reduced[5],
        reduced[6],
        reduced[7],
        reduced[12],
        reduced[8],
        reduced[9],
        reduced[10],
        reduced[13],
    )


def solution(mesh):
    placed = (
        P("dp", "seq", None),
        P("dp", "seq", None),
        P("dp", None),
        P(("dp", "seq")),
        P(("dp", "seq"), "head"),
        P(("dp", "seq"), "head"),
        P(("dp", "seq"), None),
        P(("dp", "seq"), "head"),
        P(None, "head"),
        P("head"),
        P(),
        P(),
        P("head"),
        P("head"),
        P("head"),
        P("head"),
        P("head", ("dp", "seq")),
        P(("dp", "seq"), "head"),
        P(("dp", "seq"), "head"),
        P(("dp", "seq"), "head"),
        P("head", ("dp", "seq")),
        P(("dp", "seq")),
        P(("dp", "seq"), "head"),
        P(("dp", "seq"), "head"),
        P("head", ("dp", "seq")),
    )
    return jax.shard_map(
        local,
        mesh=mesh,
        in_specs=placed,
        out_specs=(
            P("dp", "seq", None),
            P("dp", "seq", None),
            P(("dp", "seq")),
            P(("dp", "seq"), "head"),
            P(("dp", "seq"), "head"),
            P(("dp", "seq"), None),
            P(("dp", "seq"), "head"),
            P(None, "head"),
            P("head"),
            P(),
            P(),
            P("head"),
            P("head"),
            P("head"),
            P("head"),
            P("head", ("dp", "seq")),
            P(("dp", "seq"), "head"),
            P(("dp", "seq"), "head"),
            P(("dp", "seq"), "head"),
            P("head", ("dp", "seq")),
            P(("dp", "seq")),
            P(("dp", "seq"), "head"),
            P(("dp", "seq"), "head"),
            P("head", ("dp", "seq")),
        ),
        check_vma=False,
    )
```

profile of v0, /device:TPU:0, one launch (start us, length us, event | category | flops | bytes accessed | tf_op | source)
XLA Modules:
  0.0 1923.7 jit_solution(1945127162555504559)
XLA Ops:
  11.7 43.8 %all-reduce.27 = (bf16[1024]{0:T(1024)(128)(2,1)S(1)}, bf16[1024]{0:T(1024)(128)(2,1)S(1)}) all-reduce(bf16[1024]{0:T(1024)(128)(2,1)S(1)} %dynamic-update-slice.6, bf16[1024]{0:T(1024)(128)(2,1)S(1)} %dynamic-update-slice.7), channel_id=1, replica_groups=mesh['dp'=4,'seq'=4,'head'=2] {'dp','seq'}, use_global_device_ids=true, to_apply=%add.21 | all-reduce | flops 2048 | bytes 8192
  56.7 42.4 %all_gather.80 = bf16[1024,256]{1,0:T(8,128)(2,1)S(1)} all-gather(bf16[64,256]{1,0:T(8,128)(2,1)} %param.45), channel_id=1, replica_groups=mesh['dp'=4,'seq'=4,'head'=2] {'dp','seq'}, dimensions={0}, use_global_device_ids=true | all-gather | bytes 557056 | tf_op jit(solution)/shard_map/all_gather | solution.py:217
  100.5 4.2 collective-permute-start.1
  109.7 36.2 %all-gather.2 = bf16[16,64,12]{1,2,0:T(8,128)(2,1)S(1)} all-gather(bf16[1,64,12]{1,2,0:T(8,128)(2,1)} %bitcast.635), channel_id=1, replica_groups=mesh['dp'=4,'seq'=4,'head'=2] {'dp','seq'}, dimensions={0}, use_global_device_ids=true | all-gather | bytes 26112 | tf_op jit(solution)/shard_map/all_gather | solution.py:218
  159.1 10.0 all_gather.81
  169.4 46.0 %all_gather.89 = bf16[1024,256]{1,0:T(8,128)(2,1)S(1)} all-gather(bf16[64,256]{1,0:T(8,128)(2,1)S(1)} %copy-done.78), channel_id=1, replica_groups=mesh['dp'=4,'seq'=4,'head'=2] {'dp','seq'}, dimensions={0}, use_global_device_ids=true | all-gather | bytes 557056 | tf_op jit(solution)/shard_map/all_gather | solution.py:219
  216.0 40.4 %all_gather.86 = bf16[1024,64]{1,0:T(8,128)(2,1)S(1)} all-gather(bf16[64,64]{1,0:T(8,128)(2,1)S(1)} %copy-done.103), channel_id=1, replica_groups=mesh['dp'=4,'seq'=4,'head'=2] {'dp','seq'}, dimensions={0}, use_global_device_ids=true | all-gather | bytes 139264 | tf_op jit(solution)/shard_map/all_gather | solution.py:220
  257.6 40.9 %all_gather.87 = bf16[1024,64]{1,0:T(8,128)(2,1)S(1)} all-gather(bf16[64,64]{1,0:T(8,128)(2,1)S(1)} %copy-done.104), channel_id=1, replica_groups=mesh['dp'=4,'seq'=4,'head'=2] {'dp','seq'}, dimensions={0}, use_global_device_ids=true | all-gather | bytes 139264 | tf_op jit(solution)/shard_map/all_gather | solution.py:221
  299.2 13.1 all_gather.88
  315.4 39.9 %all_gather.90 = bf16[256,1024]{0,1:T(8,128)(2,1)S(1)} all-gather(bf16[256,64]{0,1:T(8,128)(2,1)S(1)} %copy-done.79), channel_id=1, replica_groups=mesh['dp'=4,'seq'=4,'head'=2] {'dp','seq'}, dimensions={1}, use_global_device_ids=true | all-gather | bytes 557056 | tf_op jit(solution)/shard_map/all_gather | solution.py:226
  372.6 13.9 all-reduce.32.cloned.1.call-done
  388.2 62.6 %all-gather.18.cloned.1.call-done = bf16[1024,1024]{1,0:T(8,128)(2,1)} async-done(((bf16[64,1024]{1,0:T(8,128)(2,1)}), bf16[1024,1024]{1,0:T(8,128)(2,1)}) %all-gather.18.cloned.1.call-update) | async-done | bytes 2097168 | tf_op jit(solution)/shard_map/all_gather | solution.py:223
  452.9 60.0 %all-gather.20.cloned.1.call-done = bf16[1024,1024]{1,0:T(8,128)(2,1)} async-done(((bf16[64,1024]{1,0:T(8,128)(2,1)}), bf16[1024,1024]{1,0:T(8,128)(2,1)}) %all-gather.20.cloned.1.call-update) | async-done | bytes 2097168 | tf_op jit(solution)/shard_map/all_gather | solution.py:224
  515.8 59.3 %all-gather.22.cloned.1.call-done = bf16[1024,1024]{0,1:T(8,128)(2,1)} async-done(((bf16[1024,64]{0,1:T(8,128)(2,1)}), bf16[1024,1024]{0,1:T(8,128)(2,1)}) %all-gather.22.cloned.1.call-update) | async-done | bytes 2097168 | tf_op jit(solution)/shard_map/all_gather | solution.py:227
  589.1 10.1 all-reduce.34.cloned.1.call-done
  620.1 4.9 while.69
  657.5 25.8 %all-gather.26.cloned.1.call-done = f32[48,64,128]{2,1,0:T(8,128)} async-done(((f32[12,64,128]{2,1,0:T(8,128)}), f32[48,64,128]{2,1,0:T(8,128)}) %all-gather.26.cloned.1.call-update) | async-done | bytes 1572880 | tf_op jit(solution)/shard_map/all_gather | solution.py:25
  686.1 5.3 while.71
  725.8 14.8 all-reduce.36.cloned.1.call-done
  743.3 4.1 collective-permute-done.3
  769.8 52.2 %reduce-scatter.40.cloned.1.call-done = f32[64,12]{1,0:T(8,128)} async-done(((f32[1024,12]{1,0:T(8,128)}), f32[64,12]{1,0:T(8,128)}) %reduce-scatter.40.cloned.1.call-update) | async-done | bytes 3088
  825.0 73.2 %all-reduce.25 = (f32[1024]{0:T(1024)S(1)}, f32[4,768]{1,0:T(4,128)}, f32[768]{0:T(1024)}, f32[4,256]{1,0:T(4,128)}, f32[256]{0:T(256)}, /*index=5*/f32[12]{0:T(...) all-reduce(f32[1024]{0:T(1024)S(1)} %get-tuple-element.561, ...), channel_id=5, replica_groups=mesh['dp'=4,'seq'=4,'head'=2] {'dp','seq'}, use_global_device_ids=true, to_apply=%region_38.39.clone | all-reduce | flops 7972 | bytes 63776
  901.5 74.6 %reduce-scatter.30.cloned.1.call-done = f32[64,64]{1,0:T(8,128)} async-done(((f32[1024,64]{1,0:T(8,128)}), f32[64,64]{1,0:T(8,128)}) %reduce-scatter.30.cloned.1.call-update) | async-done | bytes 16400 | tf_op jit(solution)/shard_map/reduce_scatter | solution.py:555
  976.1 78.9 %reduce-scatter.32.cloned.1.call-done = f32[256,64]{0,1:T(8,128)} async-done(((f32[256,1024]{0,1:T(8,128)}), f32[256,64]{0,1:T(8,128)}) %reduce-scatter.32.cloned.1.call-update) | async-done | bytes 65552 | tf_op jit(solution)/shard_map/reduce_scatter | solution.py:562
  1054.9 78.8 %reduce-scatter.26.cloned.1.call-done = f32[64,256]{1,0:T(8,128)} async-done(((f32[1024,256]{1,0:T(8,128)}), f32[64,256]{1,0:T(8,128)}) %reduce-scatter.26.cloned.1.call-update) | async-done | bytes 65552 | tf_op jit(solution)/shard_map/reduce_scatter | solution.py:549
  1133.7 78.7 %reduce-scatter.22.cloned.1.call-done = f32[64,256]{1,0:T(8,128)} async-done(((f32[1024,256]{1,0:T(8,128)}), f32[64,256]{1,0:T(8,128)}) %reduce-scatter.22.cloned.1.call-update) | async-done | bytes 65552 | tf_op jit(solution)/shard_map/reduce_scatter | solution.py:543
  1212.4 134.3 %reduce-scatter.24.cloned.1.call-done = f32[768,64]{0,1:T(8,128)} async-done(((f32[768,1024]{0,1:T(8,128)}), f32[768,64]{0,1:T(8,128)}) %reduce-scatter.24.cloned.1.call-update) | async-done | bytes 196624 | tf_op jit(solution)/shard_map/reduce_scatter | solution.py:561
  1346.7 136.6 %reduce-scatter.18.cloned.1.call-done = f32[64,768]{1,0:T(8,128)} async-done(((f32[1024,768]{1,0:T(8,128)}), f32[64,768]{1,0:T(8,128)}) %reduce-scatter.18.cloned.1.call-update) | async-done | bytes 196624 | tf_op jit(solution)/shard_map/reduce_scatter | solution.py:537
  1483.3 99.3 %reduce-scatter.34.cloned.1.call-done = f32[64,1024]{1,0:T(8,128)} async-done(((f32[1024,1024]{1,0:T(8,128)}), f32[64,1024]{1,0:T(8,128)}) %reduce-scatter.34.cloned.1.call-update) | async-done | bytes 262160 | tf_op jit(solution)/shard_map/reduce_scatter | solution.py:559
  1582.6 98.7 %reduce-scatter.36.cloned.1.call-done = f32[64,1024]{1,0:T(8,128)} async-done(((f32[1024,1024]{1,0:T(8,128)}), f32[64,1024]{1,0:T(8,128)}) %reduce-scatter.36.cloned.1.call-update) | async-done | bytes 262160 | tf_op jit(solution)/shard_map/reduce_scatter | solution.py:560
  1681.3 99.1 %reduce-scatter.38.cloned.1.call-done = f32[1024,64]{0,1:T(8,128)} async-done(((f32[1024,1024]{0,1:T(8,128)}), f32[1024,64]{0,1:T(8,128)}) %reduce-scatter.38.cloned.1.call-update) | async-done | bytes 262160 | tf_op jit(solution)/shard_map/reduce_scatter | solution.py:563
  1780.3 136.1 %reduce-scatter.20.cloned.1.call-done = f32[64,768]{1,0:T(8,128)} async-done(((f32[1024,768]{1,0:T(8,128)}), f32[64,768]{1,0:T(8,128)}) %reduce-scatter.20.cloned.1.call-update) | async-done | bytes 196624 | tf_op jit(solution)/shard_map/reduce_scatter | solution.py:540
  (563 shorter events, 202.1 us)
Async XLA Ops:
  7.2 140.8 %all-gather.12.cloned.1.call-start = ((), (), s32[]{:S(2)}) async-start(), calls=%async_computation.13 | async-start | bytes 1671168 | tf_op jit(solution)/shard_map/all_gather | solution.py:216
  8.0 348.0 %all-gather.24.cloned.1.call-start = ((), (), s32[]{:S(2)}) async-start(), calls=%async_computation.33 | async-start | bytes 1966080 | tf_op jit(solution)/shard_map/all_gather | solution.py:25
  56.7 305.5 %copy-start.62 = (f32[128]{0:T(128)}, f32[128]{0:T(128)S(1)}, u32[]{:S(2)}) copy-start(f32[128]{0:T(128)S(1)} %add_rsqrt_fusion.1) | copy-start | bytes 1540
  100.5 53.1 %collective-permute-start.1 = (f32[1,3,256]{2,1,0:T(4,128)S(1)}, f32[1,3,256]{2,1,0:T(4,128)S(1)}, u32[]{:S(2)}, u32[]{:S(2)}) collective-permute-start(f32[1,3,256]{2,1,0:T(4,128)S(1)} %slice.261), channel_id=1, source_target_pairs={{0,2},{2,4},{4,6},{1,3},{3,5},{5,7},{8,10},{10,12},{12,14},{9,11},... | collective-permute-start | bytes 9224 | tf_op jit(solution)/shard_map/ppermute | solution.py:20
  149.9 5.2 collective-permute-start
  154.5 205.1 %copy-start.15 = (f32[1,128,256]{2,1,0:T(8,128)}, f32[1,128,256]{2,1,0:T(8,128)S(1)}, u32[]{:S(2)}) copy-start(f32[1,128,256]{2,1,0:T(8,128)S(1)} %get-tuple-element.687) | copy-start | bytes 393220
  157.7 204.5 %all-gather.14.cloned.1.call-start = ((), (), s32[]{:S(2)}) async-start(), calls=%async_computation.14 | async-start | bytes 1671168 | tf_op jit(solution)/shard_map/all_gather | solution.py:215
  158.4 208.9 %all-gather.16.cloned.1.call-start = ((), (), s32[]{:S(2)}) async-start(), calls=%async_computation.15 | async-start | bytes 1671168 | tf_op jit(solution)/shard_map/all_gather | solution.py:225
  159.0 227.5 %all-reduce.32.cloned.1.call-start = ((), (), s32[]{:S(2)}) async-start(), calls=%async_computation.16 | async-start | bytes 1048576 | tf_op jit(solution)/shard_map/psum | solution.py:157
  169.2 191.0 %copy-start.125 = (f32[128,12]{0,1:T(8,128)}, f32[128,12]{0,1:T(8,128)S(1)}, u32[]{:S(2)}) copy-start(f32[128,12]{0,1:T(8,128)S(1)} %copy.212) | copy-start | bytes 18436
  169.3 190.9 %copy-start.80 = (f32[128,12]{0,1:T(8,128)}, f32[128,12]{0,1:T(8,128)S(1)}, u32[]{:S(2)}) copy-start(f32[128,12]{0,1:T(8,128)S(1)} %copy.215) | copy-start | bytes 18436
  370.3 80.6 %all-gather.18.cloned.1.call-start = ((), (), s32[]{:S(2)}) async-start(), calls=%async_computation.17 | async-start | bytes 2228224 | tf_op jit(solution)/shard_map/all_gather | solution.py:223
  370.8 142.1 %all-gather.20.cloned.1.call-start = ((), (), s32[]{:S(2)}) async-start(), calls=%async_computation.18 | async-start | bytes 2228224 | tf_op jit(solution)/shard_map/all_gather | solution.py:224
  371.6 203.5 %all-gather.22.cloned.1.call-start = ((), (), s32[]{:S(2)}) async-start(), calls=%async_computation.19 | async-start | bytes 2228224 | tf_op jit(solution)/shard_map/all_gather | solution.py:227
  372.3 226.8 %all-reduce.34.cloned.1.call-start = ((), (), s32[]{:S(2)}) async-start(), calls=%async_computation.20 | async-start | bytes 1048576 | tf_op jit(solution)/shard_map/psum | solution.py:157
  581.6 74.3 %reduce-scatter.16.cloned.1.call-start = ((), (), s32[]{:S(2)}) async-start(), calls=%async_computation.21 | async-start | bytes 327680 | tf_op jit(solution)/shard_map/reduce_scatter | solution.py:458
  625.1 58.2 %all-gather.26.cloned.1.call-start = ((), (), s32[]{:S(2)}) async-start(), calls=%async_computation.34 | async-start | bytes 1966080 | tf_op jit(solution)/shard_map/all_gather | solution.py:25
  635.7 104.9 %all-reduce.36.cloned.1.call-start = ((), (), s32[]{:S(2)}) async-start(), calls=%async_computation.36 | async-start | bytes 2359296 | tf_op jit(solution)/shard_map/psum | solution.py:157
  700.5 12.7 collective-permute-start.2
  719.1 103.0 %reduce-scatter.40.cloned.1.call-start = ((), (), s32[]{:S(2)}) async-start(), calls=%async_computation.35 | async-start | bytes 557056
  720.3 181.2 %reduce-scatter.28.cloned.1.call-start = ((), (), s32[]{:S(2)}) async-start(), calls=%async_computation.27 | async-start | bytes 557056 | tf_op jit(solution)/shard_map/reduce_scatter | solution.py:552
  721.5 254.5 %reduce-scatter.30.cloned.1.call-start = ((), (), s32[]{:S(2)}) async-start(), calls=%async_computation.28 | async-start | bytes 557056 | tf_op jit(solution)/shard_map/reduce_scatter | solution.py:555
  722.8 332.1 %reduce-scatter.32.cloned.1.call-start = ((), (), s32[]{:S(2)}) async-start(), calls=%async_computation.29 | async-start | bytes 1114112 | tf_op jit(solution)/shard_map/reduce_scatter | solution.py:562
  724.2 409.5 %reduce-scatter.26.cloned.1.call-start = ((), (), s32[]{:S(2)}) async-start(), calls=%async_computation.26 | async-start | bytes 1114112 | tf_op jit(solution)/shard_map/reduce_scatter | solution.py:549
  725.7 486.6 %reduce-scatter.22.cloned.1.call-start = ((), (), s32[]{:S(2)}) async-start(), calls=%async_computation.24 | async-start | bytes 1114112 | tf_op jit(solution)/shard_map/reduce_scatter | solution.py:543
  741.9 5.5 collective-permute-start.3
  749.0 597.7 %reduce-scatter.24.cloned.1.call-start = ((), (), s32[]{:S(2)}) async-start(), calls=%async_computation.25 | async-start | bytes 3342336 | tf_op jit(solution)/shard_map/reduce_scatter | solution.py:561
  751.6 731.7 %reduce-scatter.18.cloned.1.call-start = ((), (), s32[]{:S(2)}) async-start(), calls=%async_computation.22 | async-start | bytes 3342336 | tf_op jit(solution)/shard_map/reduce_scatter | solution.py:537
  754.9 827.7 %reduce-scatter.34.cloned.1.call-start = ((), (), s32[]{:S(2)}) async-start(), calls=%async_computation.30 | async-start | bytes 4456448 | tf_op jit(solution)/shard_map/reduce_scatter | solution.py:559
  758.5 922.7 %reduce-scatter.36.cloned.1.call-start = ((), (), s32[]{:S(2)}) async-start(), calls=%async_computation.31 | async-start | bytes 4456448 | tf_op jit(solution)/shard_map/reduce_scatter | solution.py:560
  762.3 1018.1 %reduce-scatter.38.cloned.1.call-start = ((), (), s32[]{:S(2)}) async-start(), calls=%async_computation.32 | async-start | bytes 4456448 | tf_op jit(solution)/shard_map/reduce_scatter | solution.py:563
  766.1 1150.3 %reduce-scatter.20.cloned.1.call-start = ((), (), s32[]{:S(2)}) async-start(), calls=%async_computation.23 | async-start | bytes 3342336 | tf_op jit(solution)/shard_map/reduce_scatter | solution.py:540
  (144 other events, 3678.1 us)
Sparse Core Ops, SparseCore 0:
  10.9 60.9 all-gather.11
  157.8 40.8 all-gather.23
  201.6 58.0 all-gather.13
  262.4 58.3 all-gather.15
  370.4 16.0 all-reduce.31
  389.2 61.6 all-gather.17
  453.7 59.2 all-gather.19
  515.8 59.2 all-gather.21
  581.7 17.3 all-reduce.33
  625.2 21.2 reduce-scatter.15
  648.0 35.2 all-gather.25
  719.2 21.3 all-reduce.35
  742.8 79.2 reduce-scatter.39
  824.7 74.3 reduce-scatter.27
  901.8 74.2 reduce-scatter.29
  978.8 76.1 reduce-scatter.31
  1057.6 76.0 reduce-scatter.25
  1136.4 75.9 reduce-scatter.21
  1217.9 128.7 reduce-scatter.23
  1352.1 131.1 reduce-scatter.17
  1486.2 96.3 reduce-scatter.33
  1585.5 95.7 reduce-scatter.35
  1684.1 96.1 reduce-scatter.37
  1785.8 130.6 reduce-scatter.19
where the time goes:
time: 1930 us; the launch traced here: 1920 us
  waiting for transfers between devices  1320 us (68%)
  blocking collectives  391 us (20%)
  matrix products  86.1 us (4%)
  other arithmetic  51.9 us (3%)
  local copies, waits for them, and re-layouts  41.4 us (2%)
    reduce_scatter x1, waiting for transfers between devices, local(): lax.psum_scatter(weight_grad(mixer_in, grad_gate_in), ('dp', 'seq'), scat...  137 us
    reduce_scatter x1, waiting for transfers between devices, local(): lax.psum_scatter(weight_grad(mixer_in, grad_value_ssm), ('dp', 'seq'), sc...  136 us
    reduce_scatter x1, waiting for transfers between devices, local(): lax.psum_scatter(grad_ssm_out, ('dp', 'seq'), scatter_dimension=1, tiled=...  134 us
    unnamed x2, blocking collectives  117 us
    reduce_scatter x1, waiting for transfers between devices, local(): lax.psum_scatter(grad_ffn_gate, ('dp', 'seq'), scatter_dimension=0, tiled...  99.3 us
    reduce_scatter x1, waiting for transfers between devices, local(): lax.psum_scatter(grad_ffn_down, ('dp', 'seq'), scatter_dimension=1, tiled...  99.1 us
    reduce_scatter x1, waiting for transfers between devices, local(): lax.psum_scatter(grad_ffn_up, ('dp', 'seq'), scatter_dimension=0, tiled=T...  98.7 us
    reduce_scatter x1, waiting for transfers between devices, local(): lax.psum_scatter(grad_attn_out, ('dp', 'seq'), scatter_dimension=1, tiled...  78.9 us
  transfers between devices with their start and end apart: 28, of which 20 were waited for; matrix products, arithmetic and copies ran while one was open for 6% of the time, Pallas kernels for 0%

commit v1 on v0

--- a/solution.py
+++ b/solution.py
@@ -603,6 +603,532 @@
     )
 
 
+def shift_pairs(count, step):
+    return [(i, (i + step) % count) for i in range(count)]
+
+
+def from_ahead(block, axis, step):
+    count = lax.axis_size(axis)
+    return lax.ppermute(block, axis, shift_pairs(count, -step % count))
+
+
+def to_ahead(block, axis, step):
+    return lax.ppermute(block, axis, shift_pairs(lax.axis_size(axis), step))
+
+
+def partner(block):
+    return to_ahead(block, "head", 1)
+
+
+def wrap_slice(block, start, axis):
+    size = block.shape[axis]
+    return lax.dynamic_slice_in_dim(jnp.concatenate([block, block], axis=axis), start, size, axis)
+
+
+def dot_bf(left, right, dims):
+    return lax.dot_general(
+        left.astype(jnp.bfloat16),
+        right.astype(jnp.bfloat16),
+        (dims, ((), ())),
+        preferred_element_type=jnp.float32,
+    )
+
+
+def gather_tokens(half, heads_at):
+    seqs = lax.axis_size("seq")
+    own = jnp.stack([half] + [from_ahead(half, "seq", j) for j in range(1, seqs)])
+    other = partner(own)
+    pair = jnp.where(
+        heads_at == 0, jnp.stack([own, other], axis=1), jnp.stack([other, own], axis=1)
+    )
+    return pair.reshape(-1, half.shape[-1])
+
+
+def reduce_tokens(left, weight, heads_at):
+    seqs, heads = (lax.axis_size("seq"), lax.axis_size("head"))
+    split = left.reshape(seqs, heads, -1, left.shape[-1])
+    half = split.shape[2]
+    theirs = lax.dynamic_index_in_dim(split, 1 - heads_at, 1, keepdims=False)
+    mine = lax.dynamic_index_in_dim(split, heads_at, 1, keepdims=False)
+    sent = dot_bf(theirs.reshape(seqs * half, -1), weight, ((1,), (1,))).astype(jnp.bfloat16)
+    got = partner(sent).astype(jnp.float32)
+    both = dot_bf(mine.reshape(seqs * half, -1), weight, ((1,), (1,))) + got
+    both = both.reshape(seqs, half, -1)
+    total = both[0]
+    for j in range(1, seqs):
+        total = total + to_ahead(both[j].astype(jnp.bfloat16), "seq", j).astype(jnp.float32)
+    return total
+
+
+def sum_tokens(values):
+    seqs = lax.axis_size("seq")
+    values = values + partner(values)
+    block = values.shape[0] // seqs
+    total = values
+    for j in range(1, seqs):
+        total = total + jnp.roll(from_ahead(values, "seq", j), j * block, axis=0)
+    return total
+
+
+def both_halves(half, heads_at):
+    other = partner(half)
+    return jnp.where(
+        heads_at == 0,
+        jnp.concatenate([half, other], axis=0),
+        jnp.concatenate([other, half], axis=0),
+    )
+
+
+def spread_weights(pieces):
+    rows = lax.all_to_all(pieces, "seq", 0, 0, tiled=True)
+    own = rows.reshape(-1, rows.shape[-1])
+    return jnp.concatenate(
+        [own] + [from_ahead(own, "dp", k) for k in range(1, lax.axis_size("dp"))], axis=0
+    )
+
+
+def collect_weight_grad(activation, gradient, seq_at):
+    count, seqs = (lax.axis_size("dp"), lax.axis_size("seq"))
+    chunk = activation.shape[1] // count
+    total = None
+    for k in list(range(1, count)) + [0]:
+        part = dot_bf(activation[:, k * chunk : (k + 1) * chunk], gradient, ((0,), (0,)))
+        if k:
+            part = to_ahead(part.astype(jnp.bfloat16), "dp", k).astype(jnp.float32)
+        total = part if total is None else total + part
+    rows = total.astype(jnp.bfloat16).reshape(seqs, chunk // seqs, -1)
+    found = []
+    for j in range(seqs):
+        piece = lax.dynamic_index_in_dim(rows, (seq_at - j) % seqs, 0, keepdims=False)
+        found.append(from_ahead(piece, "seq", j) if j else piece)
+    return wrap_slice(jnp.stack(found), (seqs - seq_at) % seqs, 0).astype(jnp.float32)
+
+
+def laid_out(found, first, width):
+    part = jnp.moveaxis(found[:, :, first : first + width], 0, 1)
+    return part.reshape(part.shape[0], -1)
+
+
+def sum_all(values):
+    for axis in ("dp", "seq"):
+        count = lax.axis_size(axis)
+        step = 1
+        while step < count:
+            values = values + lax.ppermute(values, axis, [(i, i ^ step) for i in range(count)])
+            step *= 2
+    return values
+
+
+def fits_whole_sequences(mesh_sizes, batch, length, parts):
+    dps, seqs, heads = mesh_sizes
+    powers = all(size & (size - 1) == 0 for size in mesh_sizes)
+    even = all(part % seqs == 0 for part in parts)
+    return powers and even and heads == 2 and batch == 1 and length * seqs <= 1024
+
+
+def whole_sequences(
+    hidden_in,
+    out_grad,
+    doc_ids,
+    mixer_gain,
+    ssm_gate_proj,
+    ssm_value_proj,
+    ssm_bc_proj,
+    ssm_step_proj,
+    conv_value_kernel,
+    conv_value_bias,
+    conv_bc_kernel,
+    conv_bc_bias,
+    decay_log,
+    step_bias,
+    skip_gain,
+    ssm_norm_gain,
+    ssm_out_proj,
+    query_proj,
+    key_proj,
+    value_proj,
+    attn_out_proj,
+    ffn_gain,
+    ffn_gate_proj,
+    ffn_up_proj,
+    ffn_down_proj,
+):
+    bf16, f32 = (jnp.bfloat16, jnp.float32)
+    dps, seqs, heads = (lax.axis_size(axis) for axis in ("dp", "seq", "head"))
+    dp_at, seq_at, head_at = (lax.axis_index(axis) for axis in ("dp", "seq", "head"))
+    _, length, width = hidden_in.shape
+    tokens = length * seqs
+    half = length // heads
+    rows = ssm_gate_proj.shape[0]
+    chunk = width // dps
+    inner = ssm_gate_proj.shape[1] // seqs
+    mheads = decay_log.shape[0] // seqs
+    hdim = inner // mheads
+    attn = query_proj.shape[1] // seqs
+    group = attn // HDIM
+    kv = key_proj.shape[1]
+    bc = ssm_bc_proj.shape[1]
+    nstate = bc // 2
+    steps = ssm_step_proj.shape[1]
+    units = ffn_gate_proj.shape[1] // seqs
+    inner_width = inner * seqs * heads
+
+    def rotated(block):
+        return wrap_slice(block, dp_at * chunk, block.ndim - 1)
+
+    def unrotated(block):
+        return wrap_slice(block, (dps - dp_at) % dps * chunk, block.ndim - 1)
+
+    def cut(block):
+        return jnp.moveaxis(block.reshape(rows, seqs, -1), 1, 0)
+
+    def same(block):
+        return jnp.broadcast_to(block[None], (seqs,) + block.shape)
+
+    def own_part(block):
+        size = block.shape[-1] // seqs
+        return lax.dynamic_slice_in_dim(block, seq_at * size, size, block.ndim - 1)
+
+    hidden_half = rotated(lax.dynamic_slice_in_dim(hidden_in[0], head_at * half, half, 0))
+    grad_half = rotated(lax.dynamic_slice_in_dim(out_grad[0], head_at * half, half, 0))
+    hidden = gather_tokens(hidden_half, head_at).astype(f32)
+    gains = lax.all_gather(
+        jnp.stack([mixer_gain, ffn_gain]), ("dp", "seq"), axis=1, tiled=True
+    )
+    gains = rotated(gains)
+    used = 2 * inner + bc + attn + 2 * kv + steps
+    padding = -used % 128
+    first_pieces = jnp.concatenate(
+        [
+            cut(ssm_gate_proj),
+            cut(ssm_value_proj),
+            same(ssm_bc_proj),
+            cut(query_proj),
+            same(key_proj),
+            same(value_proj),
+            same(ssm_step_proj),
+            jnp.zeros((seqs, rows, padding), bf16),
+        ],
+        axis=-1,
+    )
+    weight_in = spread_weights(first_pieces)
+    second_pieces = jnp.concatenate(
+        [
+            cut(ssm_out_proj.T),
+            cut(attn_out_proj.T),
+            cut(ffn_gate_proj),
+            cut(ffn_up_proj),
+            cut(ffn_down_proj.T),
+        ],
+        axis=-1,
+    )
+    weight_rest = spread_weights(second_pieces)
+    at_out = inner + attn
+    weight_out = weight_rest[:, :at_out]
+    weight_ffn = weight_rest[:, at_out : at_out + 2 * units]
+    weight_down = weight_rest[:, at_out + 2 * units :]
+
+    order = jnp.arange(tokens, dtype=jnp.int32)
+    positions = (order + seq_at * length) % tokens
+    docs = wrap_slice(doc_ids[0], seq_at * length, 0)
+    allowed = (positions[:, None] >= positions[None, :]) & (docs[:, None] == docs[None, :])
+    allowed_f32 = allowed.astype(f32)
+
+    def rms(values, gain):
+        scale = lax.rsqrt(jnp.mean(values * values, axis=-1, keepdims=True) + EPS)
+        normed = values * scale
+        return (normed, scale, (normed * gain.astype(f32)).astype(bf16))
+
+    _, _, mixer_in = rms(hidden, gains[0])
+    raw = dot_bf(mixer_in, weight_in, ((1,), (0,)))
+    at_conv = inner
+    at_query = at_conv + inner + bc
+    at_key = at_query + attn
+    at_value = at_key + kv
+    at_step = at_value + kv
+
+    gate_raw = raw[:, :inner]
+    conv_raw = raw[:, at_conv:at_query]
+    taps = conv_value_kernel.shape[0]
+    kernel = jnp.concatenate([own_part(conv_value_kernel), conv_bc_kernel], axis=-1)
+    bias = jnp.concatenate([own_part(conv_value_bias), conv_bc_bias], axis=-1)
+    masks = []
+    for k in range(taps):
+        shift = taps - 1 - k
+        masks.append(((positions >= shift) & (jnp.roll(docs, shift) == docs)).astype(f32)[:, None])
+    pre = bias
+    for k in range(taps):
+        pre = pre + kernel[k] * jnp.roll(conv_raw, taps - 1 - k, axis=0) * masks[k]
+    pre_sigma = jax.nn.sigmoid(pre)
+    act = pre * pre_sigma
+    act_value = act[:, :inner]
+    input_b = act[:, inner : inner + nstate].astype(bf16)
+    readout = act[:, inner + nstate :].astype(bf16)
+
+    step_raw = own_part(raw[:, at_step : at_step + steps])
+    step_pre = step_raw + own_part(step_bias)
+    step = jax.nn.softplus(step_pre)
+    rate = jnp.exp(own_part(decay_log))
+    log_decay = -step * rate
+    cumul = jnp.dot(allowed_f32, log_decay, precision=HIGH)
+    cumul_row = cumul.T
+
+    def per_channel(values):
+        return jnp.repeat(values, hdim, axis=-1)
+
+    def head_sums(values):
+        return jnp.sum(values.reshape(tokens, mheads, hdim), axis=-1)
+
+    skip = per_channel(own_part(skip_gain)[None])
+    stepped = (act_value * per_channel(step)).astype(bf16)
+    intersection = dot_bf(readout, input_b, ((1,), (1,)))
+
+    def decay_of(j):
+        gap = jnp.where(allowed, cumul[:, j : j + 1] - cumul_row[j : j + 1, :], 0.0)
+        return jnp.where(allowed, jnp.exp(gap), 0.0)
+
+    def columns(values, j):
+        return values[:, j * hdim : (j + 1) * hdim]
+
+    mixing = [(decay_of(j) * intersection).astype(bf16) for j in range(mheads)]
+    intra = jnp.concatenate(
+        [dot_bf(mixing[j], columns(stepped, j), ((1,), (0,))) for j in range(mheads)], axis=-1
+    )
+    ssm_y = intra + skip * act_value
+    gate_sigma = jax.nn.sigmoid(gate_raw)
+    gate_act = gate_raw * gate_sigma
+    gated = ssm_y * gate_act
+    square_sum = sum_tokens(jnp.sum(gated * gated, axis=-1, keepdims=True))
+    norm_scale = lax.rsqrt(square_sum / inner_width + EPS)
+    gated_normed = gated * norm_scale
+    norm_gain = own_part(ssm_norm_gain)
+    ssm_in = (gated_normed * norm_gain).astype(bf16)
+
+    cosine, sine = rope_tables(positions, HDIM)
+
+    def turned(values, sign):
+        return jnp.concatenate(
+            [
+                rotate(values[:, i * HDIM : (i + 1) * HDIM], cosine, sine, sign)
+                for i in range(values.shape[1] // HDIM)
+            ],
+            axis=-1,
+        )
+
+    query = turned(raw[:, at_query:at_key], 1.0).astype(bf16)
+    keys = turned(raw[:, at_key:at_value], 1.0).astype(bf16)
+    values = raw[:, at_value:at_step].astype(bf16)
+    scores_scale = HDIM ** (-0.5)
+    probs, attn_out = ([], [])
+    for i in range(group):
+        scores = dot_bf(columns(query, i), keys, ((1,), (1,))) * scores_scale
+        masked = jnp.where(allowed, scores, NEG_LARGE)
+        peak = jnp.max(masked, axis=-1, keepdims=True)
+        total = jnp.sum(jnp.where(allowed, jnp.exp(masked - peak), 0.0), axis=-1, keepdims=True)
+        log_total = peak + jnp.log(total)
+        probs.append(jnp.where(allowed, jnp.exp(scores - log_total), 0.0))
+        attn_out.append(dot_bf(probs[i], values, ((1,), (0,))))
+    attn_out = jnp.concatenate(attn_out, axis=-1)
+
+    branch_in = jnp.concatenate([ssm_in, attn_out.astype(bf16)], axis=-1)
+    mixed = hidden_half.astype(f32) + reduce_tokens(branch_in, weight_out, head_at)
+    normed_ffn, scale_ffn, ffn_half = rms(mixed, gains[1])
+    upstream = gather_tokens(grad_half, head_at)
+    ffn_in = gather_tokens(ffn_half, head_at)
+    both = dot_bf(ffn_in, weight_ffn, ((1,), (0,)))
+    gate = both[:, :units]
+    upward = both[:, units:]
+    sigma = jax.nn.sigmoid(gate)
+    hidden_act = (gate * sigma * upward).astype(bf16)
+    grad_hidden = dot_bf(upstream, weight_down, ((1,), (0,)))
+    grad_ffn = jnp.concatenate(
+        [
+            grad_hidden * upward * sigma * (1.0 + gate * (1.0 - sigma)),
+            grad_hidden * gate * sigma,
+        ],
+        axis=-1,
+    ).astype(bf16)
+
+    def rms_pull(gradient, normed, scale, gain):
+        scaled = gradient * gain.astype(f32)
+        mean = jnp.mean(scaled * normed, axis=-1, keepdims=True)
+        return (scale * (scaled - normed * mean), jnp.sum(gradient * normed, axis=0))
+
+    grad_ffn_in = reduce_tokens(grad_ffn, weight_ffn, head_at)
+    pulled, grad_ffn_gain = rms_pull(grad_ffn_in, normed_ffn, scale_ffn, gains[1])
+    grad_mixed = grad_half.astype(f32) + pulled
+    branch = gather_tokens(grad_mixed.astype(bf16), head_at)
+    block_half = mixed + reduce_tokens(hidden_act, weight_down, head_at)
+    block_out = unrotated(both_halves(block_half.astype(bf16), head_at))[None]
+
+    grad_branch = dot_bf(branch, weight_out, ((1,), (0,)))
+    grad_ssm = grad_branch[:, :inner]
+    grad_attn = grad_branch[:, inner:]
+    found_ffn = collect_weight_grad(ffn_in, grad_ffn, seq_at)
+    found_back = jnp.concatenate(
+        [
+            collect_weight_grad(upstream, hidden_act, seq_at),
+            collect_weight_grad(branch, branch_in, seq_at),
+        ],
+        axis=-1,
+    )
+
+    grad_norm_gain = jnp.sum(grad_ssm * gated_normed, axis=0)
+    scaled_grad = grad_ssm * norm_gain
+    overlap = sum_tokens(jnp.sum(scaled_grad * gated_normed, axis=-1, keepdims=True))
+
+    grad_query, grad_keys, grad_values = ([], 0.0, 0.0)
+    for i in range(group):
+        gradient = columns(grad_attn, i)
+        delta = jnp.sum(gradient * columns(attn_out, i), axis=-1, keepdims=True)
+        gradient = gradient.astype(bf16)
+        grad_values = grad_values + dot_bf(probs[i], gradient, ((0,), (0,)))
+        grad_probs = dot_bf(gradient, values, ((1,), (1,)))
+        grad_scores = (probs[i] * (grad_probs - delta) * scores_scale).astype(bf16)
+        grad_query.append(dot_bf(grad_scores, keys, ((1,), (0,))))
+        grad_keys = grad_keys + dot_bf(grad_scores, columns(query, i), ((0,), (0,)))
+    grad_query = turned(jnp.concatenate(grad_query, axis=-1), -1.0)
+    grad_keys = turned(grad_keys, -1.0)
+
+    grad_gated = norm_scale * (scaled_grad - gated_normed * (overlap / inner_width))
+    grad_y = grad_gated * gate_act
+    grad_gate_raw = grad_gated * ssm_y * gate_sigma * (1.0 + gate_raw * (1.0 - gate_sigma))
+    grad_y_round = grad_y.astype(bf16)
+    grad_stepped, grad_intersection = ([], 0.0)
+    for j in range(mheads):
+        grad_stepped.append(dot_bf(mixing[j], columns(grad_y_round, j), ((0,), (0,))))
+        grad_mixing = dot_bf(columns(grad_y_round, j), columns(stepped, j), ((1,), (1,)))
+        grad_intersection = grad_intersection + grad_mixing * decay_of(j)
+    grad_stepped = jnp.concatenate(grad_stepped, axis=-1)
+    grad_intersection = grad_intersection.astype(bf16)
+    grad_readout = dot_bf(grad_intersection, input_b, ((1,), (0,)))
+    grad_input_b = dot_bf(grad_intersection, readout, ((0,), (0,)))
+    grad_cumul = head_sums(grad_y_round.astype(f32) * intra - grad_stepped * stepped.astype(f32))
+    grad_log_decay = lax.dot_general(
+        allowed_f32, grad_cumul, (((0,), (0,)), ((), ())), precision=HIGH
+    )
+    grad_step = head_sums(grad_stepped * act_value) - grad_log_decay * rate
+    grad_decay_log = jnp.sum(grad_log_decay * log_decay, axis=0)
+    grad_step_raw = grad_step * jax.nn.sigmoid(step_pre)
+    grad_step_bias = jnp.sum(grad_step_raw, axis=0)
+    grad_skip = jnp.sum(head_sums(grad_y * act_value), axis=0)
+    grad_act = jnp.concatenate(
+        [grad_stepped * per_channel(step) + skip * grad_y, grad_input_b, grad_readout], axis=-1
+    )
+    grad_pre = grad_act * pre_sigma * (1.0 + pre * (1.0 - pre_sigma))
+    grad_bias = jnp.sum(grad_pre, axis=0)
+    grad_kernel, grad_conv_raw = ([], 0.0)
+    for k in range(taps):
+        shift = taps - 1 - k
+        masked = grad_pre * masks[k]
+        grad_kernel.append(jnp.sum(masked * jnp.roll(conv_raw, shift, axis=0), axis=0))
+        grad_conv_raw = grad_conv_raw + jnp.roll(kernel[k] * masked, -shift, axis=0)
+    grad_kernel = jnp.stack(grad_kernel)
+
+    def in_place(block, axis):
+        size = block.shape[axis]
+        shape = list(block.shape)
+        shape[axis] = size * seqs
+        return lax.dynamic_update_slice_in_dim(
+            jnp.zeros(shape, f32), block.astype(f32), seq_at * size, axis
+        )
+
+    grad_raw = jnp.concatenate(
+        [
+            grad_gate_raw,
+            grad_conv_raw,
+            grad_query,
+            grad_keys,
+            grad_values,
+            in_place(grad_step_raw, 1),
+            jnp.zeros((tokens, padding), f32),
+        ],
+        axis=-1,
+    ).astype(bf16)
+    grad_mixer_in = reduce_tokens(grad_raw, weight_in, head_at)
+    normed_pre, scale_pre, _ = rms(hidden_half.astype(f32), gains[0])
+    pulled, grad_mixer_gain = rms_pull(grad_mixer_in, normed_pre, scale_pre, gains[0])
+    hidden_grad = unrotated(both_halves(grad_mixed + pulled, head_at))[None]
+    found_in = collect_weight_grad(mixer_in, grad_raw, seq_at)
+
+    per_half = [
+        in_place(grad_kernel[:, :inner], 1).reshape(-1),
+        in_place(grad_bias[:inner], 0),
+        in_place(grad_norm_gain, 0),
+        in_place(grad_decay_log, 0),
+        in_place(grad_step_bias, 0),
+        in_place(grad_skip, 0),
+    ]
+    whole = [
+        grad_kernel[:, inner:].reshape(-1),
+        grad_bias[inner:],
+        unrotated(grad_mixer_gain),
+        unrotated(grad_ffn_gain),
+    ]
+
+    def apart(packed, like):
+        found, at = ([], 0)
+        for part in like:
+            found.append(packed[at : at + part.shape[0]])
+            at += part.shape[0]
+        return found
+
+    packed = sum_all(jnp.concatenate(per_half + whole))
+    at_whole = sum(part.shape[0] for part in per_half)
+    small = apart(packed[:at_whole], per_half)
+    shared = packed[at_whole:]
+    shared = apart(shared + partner(shared), whole)
+    grad_gains = [
+        lax.dynamic_slice_in_dim(part, (dp_at * seqs + seq_at) * rows, rows, 0)
+        for part in shared[2:]
+    ]
+
+    summed = jnp.sum(found_in, axis=0)
+    grad_bc_proj = summed[:, at_conv + inner : at_query]
+    grad_bc_proj = grad_bc_proj + partner(grad_bc_proj)
+    return (
+        block_out,
+        hidden_grad,
+        grad_gains[0],
+        laid_out(found_in, 0, inner),
+        laid_out(found_in, at_conv, inner),
+        grad_bc_proj,
+        summed[:, at_step : at_step + steps],
+        small[0].reshape(taps, -1),
+        small[1],
+        shared[0].reshape(taps, -1),
+        shared[1],
+        small[3],
+        small[4],
+        small[5],
+        small[2],
+        laid_out(found_back, units, inner).T,
+        laid_out(found_in, at_query, attn),
+        summed[:, at_key:at_value],
+        summed[:, at_value:at_step],
+        laid_out(found_back, units + inner, attn).T,
+        grad_gains[1],
+        laid_out(found_ffn, 0, units),
+        laid_out(found_ffn, units, units),
+        laid_out(found_back, 0, units).T,
+    )
+
+
+def block_step(*args):
+    hidden_in, conv_value_kernel, decay_log = (args[0], args[8], args[12])
+    batch, length, _ = hidden_in.shape
+    sizes = tuple(lax.axis_size(axis) for axis in ("dp", "seq", "head"))
+    columns = (
+        decay_log.shape[0],
+        args[17].shape[1] // HDIM,
+        args[22].shape[1],
+        conv_value_kernel.shape[1],
+    )
+    if fits_whole_sequences(sizes, batch, length, columns) and args[18].shape[1] == HDIM:
+        return whole_sequences(*args)
+    return local(*args)
+
+
 def solution(mesh):
     placed = (
         P("dp", "seq", None),
@@ -632,7 +1158,7 @@
         P("head", ("dp", "seq")),
     )
     return jax.shard_map(
-        local,
+        block_step,
         mesh=mesh,
         in_specs=placed,
         out_specs=(

time: 1930 us -> 440 us (0.23)
  waiting for transfers between devices: 1320 us -> 118 us
  blocking collectives: 391 us -> 43 us
  starting transfers between devices: 12.2 us -> 99.3 us
  matrix products: 86.1 us -> 38.6 us
  local copies, waits for them, and re-layouts: 41.4 us -> 87.4 us
    reduce_scatter x12 -> x0, waiting for transfers between devices: 1010 us -> none  [the longest x1 137 us: local(): lax.psum_scatter(weight_grad(mixer_in, grad_gate_in), ('dp', 'seq'), scat...]
    all_gather x8 -> x1, blocking collectives: 269 us -> 43 us  [whole_sequences(): lax.all_gather(jnp.stack([mixer_gain, ffn_gain]), ('dp', 'seq'), axis=1,...]
    all_gather x8 -> x0, waiting for transfers between devices: 208 us -> none  [the longest x1 62.6 us: local(): lax.all_gather(ffn_gate_proj, ('dp', 'seq'), axis=0, tiled=True)]
    unnamed x2 -> x0, blocking collectives: 117 us -> none
    ppermute x4 -> x78, waiting for transfers between devices: 4.65 us -> 109 us  [the longest x36 77.8 us: from_ahead(): return lax.ppermute(block, axis, shift_pairs(count, -step % count))]
    ppermute x4 -> x78, starting transfers between devices: 10.6 us -> 91.1 us  [the longest x36 46.4 us: from_ahead(): return lax.ppermute(block, axis, shift_pairs(count, -step % count))]
    unnamed x25 -> x0, waiting for transfers between devices: 56.3 us -> none
    dot_general x54 -> x48, matrix products: 84.9 us -> 38.6 us  [the longest x46 36 us: dot_bf(): lax.dot_general(left.astype(jnp.bfloat16), right.astype(jnp.bfloat16), (d...]
  transfers between devices with their start and end apart: 28 -> 80, of which waited for: 20 -> 34; matrix products, arithmetic and copies ran while one was open for 6% -> 35% of each run, Pallas kernels for 0% -> 0%
where the time goes in v1:
time: 440 us; the launch traced here: 434 us
  waiting for transfers between devices  118 us (27%)
  starting transfers between devices  99.3 us (23%)
  local copies, waits for them, and re-layouts  87.4 us (20%)
  other arithmetic  43.3 us (10%)
  blocking collectives  43 us (10%)
  matrix products  38.6 us (9%)
    ppermute x36, waiting for transfers between devices, from_ahead(): return lax.ppermute(block, axis, shift_pairs(count, -step % count))  77.8 us
    ppermute x36, starting transfers between devices, from_ahead(): return lax.ppermute(block, axis, shift_pairs(count, -step % count))  46.4 us
    all_gather x1, blocking collectives, whole_sequences(): lax.all_gather(jnp.stack([mixer_gain, ffn_gain]), ('dp', 'seq'), axis=1,...  43 us
    ppermute x38, starting transfers between devices, to_ahead(): return lax.ppermute(block, axis, shift_pairs(lax.axis_size(axis), step))  36.9 us
    dot_general x46, matrix products, dot_bf(): lax.dot_general(left.astype(jnp.bfloat16), right.astype(jnp.bfloat16), (d...  36 us
    ppermute x38, waiting for transfers between devices, to_ahead(): return lax.ppermute(block, axis, shift_pairs(lax.axis_size(axis), step))  27 us
    unnamed x348, local copies, waits for them, and re-layouts  17.8 us
    concatenate x6, local copies, waits for them, and re-layouts, whole_sequences(): jnp.concatenate([grad_gate_raw, grad_conv_raw, grad_query, grad_keys, gra...  12.9 us
  transfers between devices with their start and end apart: 80, of which 34 were waited for; matrix products, arithmetic and copies ran while one was open for 35% of the time, Pallas kernels for 0%

profile of v1, /device:TPU:0, one launch (start us, length us, event | category | flops | bytes accessed | tf_op | source)
XLA Modules:
  0.0 433.8 jit_solution(3173942856427777827)
XLA Ops:
  2.3 5.1 %collective-permute-start = (bf16[64,1024]{1,0:T(8,128)(2,1)S(1)}, bf16[64,1024]{1,0:T(8,128)(2,1)S(1)}, u32[]{:S(2)}, u32[]{:S(2)}) collective-permute-start(bf16[64,1024]{1,0:T(8,128)(2,1)S(1)} %get-tuple-element.210), channel_id=1, source_target_pairs={{0,6},{2,0},{4,2},{6,4},{1,7},{3,1},{5,3},{7,5},{8,14},{10,8},{12,... | collective-permute-start | bytes 393224 | tf_op jit(solution)/shard_map/ppermute | solution.py:612
  18.0 4.1 all-to-all-start
  22.2 43.0 %all-gather = bf16[16,64,2]{1,2,0:T(2,128)(2,1)S(1)} all-gather(bf16[1,64,2]{1,2,0:T(2,128)(2,1)S(1)} %maximum_bitcast_fusion), channel_id=1, replica_groups=mesh['dp'=4,'seq'=4,'head'=2] {'dp','seq'}, dimensions={0}, use_global_device_ids=true | all-gather | bytes 4352 | tf_op jit(solution)/shard_map/all_gather | solution.py:795
  82.7 4.1 all-to-all-start.1
  92.8 9.1 %all-to-all-done.1 = bf16[4,64,1024]{2,1,0:T(8,128)(2,1)} async-done(((bf16[4,64,1024]{2,1,0:T(8,128)(2,1)}), bf16[4,64,1024]{2,1,0:T(8,128)(2,1)}, u32[]{:S(2)}, u32[]{:S(2)}) %all-to-all-start.1) | async-done | bytes 524320 | tf_op jit(solution)/shard_map/all_to_all | solution.py:683
  103.4 8.0 %collective-permute-done.5 = bf16[256,896]{1,0:T(8,128)(2,1)} collective-permute-done((bf16[256,896]{1,0:T(8,128)(2,1)}, bf16[256,896]{1,0:T(8,128)(2,1)}, u32[]{:S(2)}, u32[]{:S(2)}) %collective-permute-start.5) | collective-permute-done | bytes 458784 | tf_op jit(solution)/shard_map/ppermute | solution.py:612
  133.4 3.4 fusion.170
  148.6 3.2 collective-permute-done.10
  152.4 10.2 %collective-permute-done.13 = bf16[256,1024]{1,0:T(8,128)(2,1)S(1)} collective-permute-done((bf16[256,1024]{1,0:T(8,128)(2,1)}, bf16[256,1024]{1,0:T(8,128)(2,1)S(1)}, u32[]{:S(2)}, u32[]{:S(2)}) %collective-permute-start.13) | collective-permute-done | bytes 524320 | tf_op jit(solution)/shard_map/ppermute | solution.py:612
  171.7 4.2 collective-permute-done.15
  175.9 4.8 %collective-permute-done.16 = bf16[64,1024]{1,0:T(8,128)(2,1)S(1)} collective-permute-done((bf16[64,1024]{1,0:T(8,128)(2,1)S(1)}, bf16[64,1024]{1,0:T(8,128)(2,1)S(1)}, u32[]{:S(2)}, u32[]{:S(2)}) %collective-permute-start.16) | collective-permute-done | bytes 131104 | tf_op jit(solution)/shard_map/ppermute | solution.py:616
  181.0 3.1 collective-permute-start.18
  188.0 9.6 %collective-permute-done.19 = bf16[64,1024]{1,0:T(8,128)(2,1)S(1)} collective-permute-done((bf16[64,1024]{1,0:T(8,128)(2,1)S(1)}, bf16[64,1024]{1,0:T(8,128)(2,1)S(1)}, u32[]{:S(2)}, u32[]{:S(2)}) %collective-permute-start.19) | collective-permute-done | bytes 131104 | tf_op jit(solution)/shard_map/ppermute | solution.py:612
  218.4 3.6 collective-permute-done.75
  222.7 4.1 collective-permute-done.76
  226.8 5.7 %collective-permute-done.77 = bf16[64,256]{1,0:T(8,128)(2,1)S(1)} collective-permute-done((bf16[64,256]{1,0:T(8,128)(2,1)S(1)}, bf16[64,256]{1,0:T(8,128)(2,1)S(1)}, u32[]{:S(2)}, u32[]{:S(2)}) %collective-permute-start.77) | collective-permute-done | bytes 32800 | tf_op jit(solution)/shard_map/ppermute | solution.py:612
  237.5 4.5 %collective-permute-done.70 = bf16[64,512]{1,0:T(8,128)(2,1)S(1)} collective-permute-done((bf16[64,512]{1,0:T(8,128)(2,1)S(1)}, bf16[64,512]{1,0:T(8,128)(2,1)S(1)}, u32[]{:S(2)}, u32[]{:S(2)}) %collective-permute-start.70) | collective-permute-done | bytes 65568 | tf_op jit(solution)/shard_map/ppermute | solution.py:612
  246.6 4.3 collective-permute-done.32
  250.9 3.6 collective-permute-done.33
  255.5 3.9 collective-permute-start.35
  263.3 7.4 %collective-permute-done.36 = bf16[64,1024]{1,0:T(8,128)(2,1)S(1)} collective-permute-done((bf16[64,1024]{1,0:T(8,128)(2,1)S(1)}, bf16[64,1024]{1,0:T(8,128)(2,1)S(1)}, u32[]{:S(2)}, u32[]{:S(2)}) %collective-permute-start.36) | collective-permute-done | bytes 131104 | tf_op jit(solution)/shard_map/ppermute | solution.py:612
  309.0 3.3 multiply_reduce_fusion.5
  334.4 3.2 concatenate.241
  343.1 3.6 concatenate.234
  349.5 3.0 convolution_convert_fusion.3
  357.2 4.1 collective-permute-start.63
  365.5 4.8 %collective-permute-done.64 = bf16[64,256]{1,0:T(8,128)(2,1)S(1)} collective-permute-done((bf16[64,256]{1,0:T(8,128)(2,1)S(1)}, bf16[64,256]{1,0:T(8,128)(2,1)S(1)}, u32[]{:S(2)}, u32[]{:S(2)}) %collective-permute-start.64) | collective-permute-done | bytes 32800 | tf_op jit(solution)/shard_map/ppermute | solution.py:612
  370.4 5.7 %collective-permute-done.65 = bf16[64,256]{1,0:T(8,128)(2,1)S(1)} collective-permute-done((bf16[64,256]{1,0:T(8,128)(2,1)S(1)}, bf16[64,256]{1,0:T(8,128)(2,1)S(1)}, u32[]{:S(2)}, u32[]{:S(2)}) %collective-permute-start.65) | collective-permute-done | bytes 32800 | tf_op jit(solution)/shard_map/ppermute | solution.py:612
  388.1 8.4 %collective-permute-start.44 = (bf16[64,1024]{1,0:T(8,128)(2,1)S(1)}, bf16[64,1024]{1,0:T(8,128)(2,1)S(1)}, u32[]{:S(2)}, u32[]{:S(2)}) collective-permute-start(bf16[64,1024]{1,0:T(8,128)(2,1)S(1)} %get-tuple-element.244), channel_id=1, source_target_pairs={{0,2},{2,4},{4,6},{6,0},{1,3},{3,5},{5,7},{7,1},{8,10},{10,12},{12... | collective-permute-start | bytes 393224 | tf_op jit(solution)/shard_map/ppermute | solution.py:616
  400.0 3.7 collective-permute-start.25
  416.7 3.4 collective-permute-start.50
  422.0 3.4 collective-permute-start.51
  (751 shorter events, 234.3 us)
Async XLA Ops:
  2.3 66.4 %collective-permute-start = (bf16[64,1024]{1,0:T(8,128)(2,1)S(1)}, bf16[64,1024]{1,0:T(8,128)(2,1)S(1)}, u32[]{:S(2)}, u32[]{:S(2)}) collective-permute-start(bf16[64,1024]{1,0:T(8,128)(2,1)S(1)} %get-tuple-element.210), channel_id=1, source_target_pairs={{0,6},{2,0},{4,2},{6,4},{1,7},{3,1},{5,3},{7,5},{8,14},{10,8},{12,... | collective-permute-start | bytes 393224 | tf_op jit(solution)/shard_map/ppermute | solution.py:612
  7.4 70.3 %collective-permute-start.1 = (bf16[64,1024]{1,0:T(8,128)(2,1)S(1)}, bf16[64,1024]{1,0:T(8,128)(2,1)S(1)}, u32[]{:S(2)}, u32[]{:S(2)}) collective-permute-start(bf16[64,1024]{1,0:T(8,128)(2,1)S(1)} %get-tuple-element.210), channel_id=1, source_target_pairs={{0,4},{2,6},{4,0},{6,2},{1,5},{3,7},{5,1},{7,3},{8,12},{10,14},{12... | collective-permute-start | bytes 393224 | tf_op jit(solution)/shard_map/ppermute | solution.py:612
  7.4 70.3 %collective-permute-start.2 = (bf16[64,1024]{1,0:T(8,128)(2,1)S(1)}, bf16[64,1024]{1,0:T(8,128)(2,1)S(1)}, u32[]{:S(2)}, u32[]{:S(2)}) collective-permute-start(bf16[64,1024]{1,0:T(8,128)(2,1)S(1)} %get-tuple-element.210), channel_id=1, source_target_pairs={{0,2},{2,4},{4,6},{6,0},{1,3},{3,5},{5,7},{7,1},{8,10},{10,12},{12... | collective-permute-start | bytes 393224 | tf_op jit(solution)/shard_map/ppermute | solution.py:612
  9.5 68.3 %collective-permute-start.27 = (bf16[64,1024]{1,0:T(8,128)(2,1)S(1)}, bf16[64,1024]{1,0:T(8,128)(2,1)S(1)}, u32[]{:S(2)}, u32[]{:S(2)}) collective-permute-start(bf16[64,1024]{1,0:T(8,128)(2,1)S(1)} %fusion.72), channel_id=1, source_target_pairs={{0,6},{2,0},{4,2},{6,4},{1,7},{3,1},{5,3},{7,5},{8,14},{10,8},{12,... | collective-permute-start | bytes 393224 | tf_op jit(solution)/shard_map/ppermute | solution.py:612
  12.4 65.5 %collective-permute-start.28 = (bf16[64,1024]{1,0:T(8,128)(2,1)S(1)}, bf16[64,1024]{1,0:T(8,128)(2,1)S(1)}, u32[]{:S(2)}, u32[]{:S(2)}) collective-permute-start(bf16[64,1024]{1,0:T(8,128)(2,1)S(1)} %fusion.72), channel_id=1, source_target_pairs={{0,4},{2,6},{4,0},{6,2},{1,5},{3,7},{5,1},{7,3},{8,12},{10,14},{12... | collective-permute-start | bytes 393224 | tf_op jit(solution)/shard_map/ppermute | solution.py:612
  18.0 64.7 %all-to-all-start = ((bf16[4,64,896]{2,1,0:T(8,128)(2,1)}), bf16[4,64,896]{2,1,0:T(8,128)(2,1)}, u32[]{:S(2)}, u32[]{:S(2)}) async-start(bf16[4,64,896]{2,1,0:T(8,128)(2,1)} %concatenate.192), calls=%async_computation | async-start | bytes 917504 | tf_op jit(solution)/shard_map/all_to_all | solution.py:683
  82.7 19.2 %all-to-all-start.1 = ((bf16[4,64,1024]{2,1,0:T(8,128)(2,1)}), bf16[4,64,1024]{2,1,0:T(8,128)(2,1)}, u32[]{:S(2)}, u32[]{:S(2)}) async-start(bf16[4,64,1024]{2,1,0:T(8,128)(2,1)} %copy.315), calls=%async_computation.1 | async-start | bytes 1048576 | tf_op jit(solution)/shard_map/all_to_all | solution.py:683
  89.6 13.7 %collective-permute-start.4 = (bf16[256,896]{1,0:T(8,128)(2,1)}, bf16[256,896]{1,0:T(8,128)(2,1)}, u32[]{:S(2)}, u32[]{:S(2)}) collective-permute-start(bf16[256,896]{1,0:T(8,128)(2,1)} %bitcast.18), channel_id=1, source_target_pairs={{0,24},{8,0},{16,8},{24,16},{1,25},{9,1},{17,9},{25,17},{2,26},{10... | collective-permute-start | bytes 1376264 | tf_op jit(solution)/shard_map/ppermute | solution.py:612
  89.7 21.7 %collective-permute-start.5 = (bf16[256,896]{1,0:T(8,128)(2,1)}, bf16[256,896]{1,0:T(8,128)(2,1)}, u32[]{:S(2)}, u32[]{:S(2)}) collective-permute-start(bf16[256,896]{1,0:T(8,128)(2,1)} %bitcast.18), channel_id=1, source_target_pairs={{0,16},{8,24},{16,0},{24,8},{1,17},{9,25},{17,1},{25,9},{2,18},{10... | collective-permute-start | bytes 1376264 | tf_op jit(solution)/shard_map/ppermute | solution.py:612
  90.4 22.9 %collective-permute-start.6 = (bf16[256,896]{1,0:T(8,128)(2,1)}, bf16[256,896]{1,0:T(8,128)(2,1)}, u32[]{:S(2)}, u32[]{:S(2)}) collective-permute-start(bf16[256,896]{1,0:T(8,128)(2,1)} %bitcast.18), channel_id=1, source_target_pairs={{0,8},{8,16},{16,24},{24,0},{1,9},{9,17},{17,25},{25,1},{2,10},{10... | collective-permute-start | bytes 1376264 | tf_op jit(solution)/shard_map/ppermute | solution.py:612
  101.9 50.3 %collective-permute-start.11 = (bf16[256,1024]{1,0:T(8,128)(2,1)}, bf16[256,1024]{1,0:T(8,128)(2,1)}, u32[]{:S(2)}, u32[]{:S(2)}) collective-permute-start(bf16[256,1024]{1,0:T(8,128)(2,1)} %bitcast.43), channel_id=1, source_target_pairs={{0,24},{8,0},{16,8},{24,16},{1,25},{9,1},{17,9},{25,17},{2,26},{10... | collective-permute-start | bytes 1572872 | tf_op jit(solution)/shard_map/ppermute | solution.py:612
  102.0 50.1 %collective-permute-start.12 = (bf16[256,1024]{1,0:T(8,128)(2,1)}, bf16[256,1024]{1,0:T(8,128)(2,1)}, u32[]{:S(2)}, u32[]{:S(2)}) collective-permute-start(bf16[256,1024]{1,0:T(8,128)(2,1)} %bitcast.43), channel_id=1, source_target_pairs={{0,16},{8,24},{16,0},{24,8},{1,17},{9,25},{17,1},{25,9},{2,18},{10... | collective-permute-start | bytes 1572872 | tf_op jit(solution)/shard_map/ppermute | solution.py:612
  148.5 14.1 %collective-permute-start.13 = (bf16[256,1024]{1,0:T(8,128)(2,1)}, bf16[256,1024]{1,0:T(8,128)(2,1)S(1)}, u32[]{:S(2)}, u32[]{:S(2)}) collective-permute-start(bf16[256,1024]{1,0:T(8,128)(2,1)} %bitcast.43), channel_id=1, source_target_pairs={{0,8},{8,16},{16,24},{24,0},{1,9},{9,17},{17,25},{25,1},{2,10},{10... | collective-permute-start | bytes 1572872 | tf_op jit(solution)/shard_map/ppermute | solution.py:612
  184.0 13.6 %collective-permute-start.19 = (bf16[64,1024]{1,0:T(8,128)(2,1)S(1)}, bf16[64,1024]{1,0:T(8,128)(2,1)S(1)}, u32[]{:S(2)}, u32[]{:S(2)}) collective-permute-start(bf16[64,1024]{1,0:T(8,128)(2,1)S(1)} %multiply_convert_fusion.9), channel_id=1, source_target_pairs={{0,4},{2,6},{4,0},{6,2},{1,5},{3,7},{5,1},{7,3},{8,12},{10,14},{12... | collective-permute-start | bytes 393224 | tf_op jit(solution)/shard_map/ppermute | solution.py:612
  212.0 20.6 %collective-permute-start.66 = (bf16[256,512]{1,0:T(8,128)(2,1)S(1)}, bf16[256,512]{1,0:T(8,128)(2,1)S(1)}, u32[]{:S(2)}, u32[]{:S(2)}) collective-permute-start(bf16[256,512]{1,0:T(8,128)(2,1)S(1)} %convolution_convert_fusion.9), channel_id=1, source_target_pairs={{0,8},{8,16},{16,24},{24,0},{1,9},{9,17},{17,25},{25,1},{2,10},{10... | collective-permute-start | bytes 786440 | tf_op jit(solution)/shard_map/ppermute | solution.py:616
  212.0 20.6 %collective-permute-start.67 = (bf16[256,512]{1,0:T(8,128)(2,1)S(1)}, bf16[256,512]{1,0:T(8,128)(2,1)S(1)}, u32[]{:S(2)}, u32[]{:S(2)}) collective-permute-start(bf16[256,512]{1,0:T(8,128)(2,1)S(1)} %convolution_convert_fusion.8), channel_id=1, source_target_pairs={{0,16},{8,24},{16,0},{24,8},{1,17},{9,25},{17,1},{25,9},{2,18},{10... | collective-permute-start | bytes 786440 | tf_op jit(solution)/shard_map/ppermute | solution.py:616
  215.1 17.5 %collective-permute-start.68 = (bf16[256,512]{1,0:T(8,128)(2,1)S(1)}, bf16[256,512]{1,0:T(8,128)(2,1)S(1)}, u32[]{:S(2)}, u32[]{:S(2)}) collective-permute-start(bf16[256,512]{1,0:T(8,128)(2,1)S(1)} %convolution_convert_fusion.7), channel_id=1, source_target_pairs={{0,24},{8,0},{16,8},{24,16},{1,25},{9,1},{17,9},{25,17},{2,26},{10... | collective-permute-start | bytes 786440 | tf_op jit(solution)/shard_map/ppermute | solution.py:616
  217.1 25.0 %collective-permute-start.31 = (bf16[256,1024]{1,0:T(8,128)(2,1)S(1)}, bf16[256,1024]{1,0:T(8,128)(2,1)S(1)}, u32[]{:S(2)}, u32[]{:S(2)}) collective-permute-start(bf16[256,1024]{1,0:T(8,128)(2,1)S(1)} %convolution_convert_fusion), channel_id=1, source_target_pairs={{0,1},{1,0},{2,3},{3,2},{4,5},{5,4},{6,7},{7,6},{8,9},{9,8},{10,11... | collective-permute-start | bytes 1572872 | tf_op jit(solution)/shard_map/ppermute | solution.py:616
  232.5 38.4 %collective-permute-start.22 = (bf16[256,1024]{1,0:T(8,128)(2,1)S(1)}, bf16[256,1024]{1,0:T(8,128)(2,1)S(1)}, u32[]{:S(2)}, u32[]{:S(2)}) collective-permute-start(bf16[256,1024]{1,0:T(8,128)(2,1)S(1)} %convolution_convert_fusion.1), channel_id=1, source_target_pairs={{0,1},{1,0},{2,3},{3,2},{4,5},{5,4},{6,7},{7,6},{8,9},{9,8},{10,11... | collective-permute-start | bytes 1572872 | tf_op jit(solution)/shard_map/ppermute | solution.py:616
  272.9 152.4 %collective-permute-start.23 = (bf16[64,1024]{1,0:T(8,128)(2,1)}, bf16[64,1024]{1,0:T(8,128)(2,1)}, u32[]{:S(2)}, u32[]{:S(2)}) collective-permute-start(bf16[64,1024]{1,0:T(8,128)(2,1)} %get-tuple-element.256), channel_id=1, source_target_pairs={{0,2},{2,4},{4,6},{6,0},{1,3},{3,5},{5,7},{7,1},{8,10},{10,12},{12... | collective-permute-start | bytes 393224 | tf_op jit(solution)/shard_map/ppermute | solution.py:616
  286.9 65.8 %collective-permute-start.60 = (bf16[256,256]{1,0:T(8,128)(2,1)}, bf16[256,256]{1,0:T(8,128)(2,1)}, u32[]{:S(2)}, u32[]{:S(2)}) collective-permute-start(bf16[256,256]{1,0:T(8,128)(2,1)} %convolution_convert_fusion.15), channel_id=1, source_target_pairs={{0,8},{8,16},{16,24},{24,0},{1,9},{9,17},{17,25},{25,1},{2,10},{10... | collective-permute-start | bytes 393224 | tf_op jit(solution)/shard_map/ppermute | solution.py:616
  289.5 18.1 %collective-permute-start.41 = (f32[512,1]{0,1:T(1,128)}, f32[512,1]{0,1:T(1,128)}, u32[]{:S(2)}, u32[]{:S(2)}) collective-permute-start(f32[512,1]{0,1:T(1,128)} %add.481), channel_id=1, source_target_pairs={{0,4},{2,6},{4,0},{6,2},{1,5},{3,7},{5,1},{7,3},{8,12},{10,14},{12... | collective-permute-start | bytes 6152 | tf_op jit(solution)/shard_map/ppermute | solution.py:612
  291.3 12.1 %collective-permute-start.40 = (f32[512,1]{0,1:T(1,128)}, f32[512,1]{0,1:T(1,128)}, u32[]{:S(2)}, u32[]{:S(2)}) collective-permute-start(f32[512,1]{0,1:T(1,128)} %add.481), channel_id=1, source_target_pairs={{0,6},{2,0},{4,2},{6,4},{1,7},{3,1},{5,3},{7,5},{8,14},{10,8},{12,... | collective-permute-start | bytes 6152 | tf_op jit(solution)/shard_map/ppermute | solution.py:612
  303.3 50.6 %collective-permute-start.61 = (bf16[256,256]{1,0:T(8,128)(2,1)}, bf16[256,256]{1,0:T(8,128)(2,1)}, u32[]{:S(2)}, u32[]{:S(2)}) collective-permute-start(bf16[256,256]{1,0:T(8,128)(2,1)} %convolution_convert_fusion.14), channel_id=1, source_target_pairs={{0,16},{8,24},{16,0},{24,8},{1,17},{9,25},{17,1},{25,9},{2,18},{10... | collective-permute-start | bytes 393224 | tf_op jit(solution)/shard_map/ppermute | solution.py:616
  305.4 50.4 %collective-permute-start.62 = (bf16[256,256]{1,0:T(8,128)(2,1)}, bf16[256,256]{1,0:T(8,128)(2,1)}, u32[]{:S(2)}, u32[]{:S(2)}) collective-permute-start(bf16[256,256]{1,0:T(8,128)(2,1)} %convolution_convert_fusion.13), channel_id=1, source_target_pairs={{0,24},{8,0},{16,8},{24,16},{1,25},{9,1},{17,9},{25,17},{2,26},{10... | collective-permute-start | bytes 393224 | tf_op jit(solution)/shard_map/ppermute | solution.py:616
  341.4 36.8 %collective-permute-start.53 = (bf16[256,896]{1,0:T(8,128)(2,1)}, bf16[256,896]{1,0:T(8,128)(2,1)}, u32[]{:S(2)}, u32[]{:S(2)}) collective-permute-start(bf16[256,896]{1,0:T(8,128)(2,1)} %convolution_convert_fusion.6), channel_id=1, source_target_pairs={{0,8},{8,16},{16,24},{24,0},{1,9},{9,17},{17,25},{25,1},{2,10},{10... | collective-permute-start | bytes 1376264 | tf_op jit(solution)/shard_map/ppermute | solution.py:616
  352.7 25.5 %collective-permute-start.54 = (bf16[256,896]{1,0:T(8,128)(2,1)}, bf16[256,896]{1,0:T(8,128)(2,1)}, u32[]{:S(2)}, u32[]{:S(2)}) collective-permute-start(bf16[256,896]{1,0:T(8,128)(2,1)} %convolution_convert_fusion.5), channel_id=1, source_target_pairs={{0,16},{8,24},{16,0},{24,8},{1,17},{9,25},{17,1},{25,9},{2,18},{10... | collective-permute-start | bytes 1376264 | tf_op jit(solution)/shard_map/ppermute | solution.py:616
  354.0 24.2 %collective-permute-start.55 = (bf16[256,896]{1,0:T(8,128)(2,1)S(1)}, bf16[256,896]{1,0:T(8,128)(2,1)}, u32[]{:S(2)}, u32[]{:S(2)}) collective-permute-start(bf16[256,896]{1,0:T(8,128)(2,1)S(1)} %copy-done.54), channel_id=1, source_target_pairs={{0,24},{8,0},{16,8},{24,16},{1,25},{9,1},{17,9},{25,17},{2,26},{10... | collective-permute-start | bytes 1376264 | tf_op jit(solution)/shard_map/ppermute | solution.py:616
  378.2 47.2 %collective-permute-start.24 = (bf16[64,1024]{1,0:T(8,128)(2,1)}, bf16[64,1024]{1,0:T(8,128)(2,1)}, u32[]{:S(2)}, u32[]{:S(2)}) collective-permute-start(bf16[64,1024]{1,0:T(8,128)(2,1)} %get-tuple-element.258), channel_id=1, source_target_pairs={{0,4},{2,6},{4,0},{6,2},{1,5},{3,7},{5,1},{7,3},{8,12},{10,14},{12... | collective-permute-start | bytes 393224 | tf_op jit(solution)/shard_map/ppermute | solution.py:616
  380.6 17.7 %collective-permute-start.57 = (bf16[64,896]{1,0:T(8,128)(2,1)S(1)}, bf16[64,896]{1,0:T(8,128)(2,1)S(1)}, u32[]{:S(2)}, u32[]{:S(2)}) collective-permute-start(bf16[64,896]{1,0:T(8,128)(2,1)S(1)} %get-tuple-element.268), channel_id=1, source_target_pairs={{0,4},{2,6},{4,0},{6,2},{1,5},{3,7},{5,1},{7,3},{8,12},{10,14},{12... | collective-permute-start | bytes 344072 | tf_op jit(solution)/shard_map/ppermute | solution.py:612
  383.1 15.3 %collective-permute-start.58 = (bf16[64,896]{1,0:T(8,128)(2,1)S(1)}, bf16[64,896]{1,0:T(8,128)(2,1)S(1)}, u32[]{:S(2)}, u32[]{:S(2)}) collective-permute-start(bf16[64,896]{1,0:T(8,128)(2,1)S(1)} %get-tuple-element.266), channel_id=1, source_target_pairs={{0,2},{2,4},{4,6},{6,0},{1,3},{3,5},{5,7},{7,1},{8,10},{10,12},{12... | collective-permute-start | bytes 344072 | tf_op jit(solution)/shard_map/ppermute | solution.py:612
  400.0 25.3 %collective-permute-start.25 = (bf16[64,1024]{1,0:T(8,128)(2,1)S(1)}, bf16[64,1024]{1,0:T(8,128)(2,1)S(1)}, u32[]{:S(2)}, u32[]{:S(2)}) collective-permute-start(bf16[64,1024]{1,0:T(8,128)(2,1)S(1)} %copy-done.71), channel_id=1, source_target_pairs={{0,6},{2,0},{4,2},{6,4},{1,7},{3,1},{5,3},{7,5},{8,14},{10,8},{12,... | collective-permute-start | bytes 393224 | tf_op jit(solution)/shard_map/ppermute | solution.py:616
  (204 other events, 1829.5 us)

commit v2 on v0

--- a/solution.py
+++ b/solution.py
@@ -3,6 +3,8 @@
 import jax
 import jax.numpy as jnp
 from jax import lax
+from jax.experimental import pallas as pl
+from jax.experimental.pallas import tpu as pltpu
 from jax.sharding import PartitionSpec as P
 
 HDIM = 64
@@ -603,6 +605,1077 @@
     )
 
 
+ROWS = 128
+
+
+def mm(left, right, on_left, on_right):
+    return lax.dot_general(
+        left, right, (((on_left,), (on_right,)), ((), ())), preferred_element_type=jnp.float32
+    )
+
+
+def exact_mm(mask, values, on_mask):
+    total = None
+    for _ in range(3):
+        part = values.astype(jnp.bfloat16)
+        values = values - part.astype(jnp.float32)
+        term = mm(mask, part, on_mask, 0)
+        total = term if total is None else total + term
+    return total
+
+
+def sigmoid(values):
+    return 1.0 / (1.0 + jnp.exp(-values))
+
+
+def local_call(body, out_shape, scratch, args):
+    windowed = any(isinstance(arg, Window) for arg in args)
+
+    def whole(arg):
+        if not windowed:
+            return pl.BlockSpec(memory_space=pltpu.VMEM)
+        return pl.BlockSpec(arg.shape, lambda _: (0, 0))
+
+    def spec(arg):
+        if arg.ndim == 1:
+            return pl.BlockSpec(memory_space=pltpu.SMEM)
+        if isinstance(arg, Window):
+            block = arg.block
+            return pl.BlockSpec(arg.shape, lambda _: (0, block))
+        return whole(arg)
+
+    return pl.pallas_call(
+        body,
+        out_shape=out_shape,
+        in_specs=[spec(arg) for arg in args],
+        out_specs=[whole(out) for out in out_shape],
+        scratch_shapes=scratch,
+        grid=(1,) if windowed else (),
+    )(*(arg.array if isinstance(arg, Window) else arg for arg in args))
+
+
+def shape_of(rows, columns, dtype=jnp.float32):
+    return jax.ShapeDtypeStruct((rows, columns), dtype)
+
+
+class Layout:
+    def __init__(self, tokens, width, inner, nstate, kv, heads, taps, inner_width):
+        self.tokens, self.width, self.inner, self.nstate = (tokens, width, inner, nstate)
+        self.kv, self.heads, self.taps, self.inner_width = (kv, heads, taps, inner_width)
+        self.hdim = inner // heads
+        self.value = 2 * nstate
+        self.attn_value = self.value + inner
+        self.gate = self.attn_value + kv
+        self.step = self.gate + inner
+        self.gain = self.step + heads
+        self.query = -(-(self.gain + 2) // 128) * 128
+        self.total = self.query + 2 * kv
+        self.step_tile = self.step // 128 * 128
+        self.step_lane = self.step - self.step_tile
+
+
+def put_pieces(target, pieces, head, half):
+    count = len(pieces) // 2
+    for j in range(count):
+        own = pl.multiple_of((2 * j + head) * half, half)
+        other = pl.multiple_of((2 * j + 1 - head) * half, half)
+        target[pl.ds(own, half), :] = pieces[j][...]
+        target[pl.ds(other, half), :] = pieces[count + j][...]
+
+
+def split_product(left, weights, sent, mine, head, half):
+    seqs = left.shape[0] // (2 * half)
+
+    def rows_of(side):
+        starts = [pl.multiple_of((2 * j + side) * half, half) for j in range(seqs)]
+        return jnp.concatenate([left[pl.ds(start, half), :] for start in starts], axis=0)
+
+    theirs, own = (rows_of(1 - head), rows_of(head))
+    at = 0
+    for weight in weights:
+        columns = slice(at, at + weight.shape[0])
+        at += weight.shape[0]
+        sent[:, columns] = mm(theirs, weight[...], 1, 1).astype(sent.dtype)
+        mine[:, columns] = mm(own, weight[...], 1, 1)
+
+
+def times_pieces(left, weights):
+    total, at = (None, 0)
+    for weight in weights:
+        size = weight.shape[0]
+        term = mm(left[:, at : at + size], weight[...], 1, 0)
+        total = term if total is None else total + term
+        at += size
+    return total
+
+
+class Window:
+    def __init__(self, array, first, width):
+        self.array, self.block, self.shape = (array, first // width, (array.shape[0], width))
+        self.ndim = 2
+
+
+def window(array, first, width):
+    if first % width == 0 and width % 128 == 0:
+        return Window(array, first, width)
+    return array[:, first : first + width]
+
+
+def allowed_rows(meta, meta_column, start):
+    column = meta_column[pl.ds(start, ROWS), :]
+    return (column[:, 0:1] >= meta[0:1, :]) & (column[:, 1:2] == meta[1:2, :])
+
+
+def conv_tile(raw, params, column, at, taps):
+    source = raw[:, at : at + 128]
+    pre = params[taps : taps + 1, at : at + 128]
+    for k in range(taps):
+        shift = taps - 1 - k
+        moved = pltpu.roll(source, shift, 0) if shift else source
+        pre = pre + params[k : k + 1, at : at + 128] * moved * column[:, 2 + k : 3 + k]
+    return (source, pre)
+
+
+def over_channels(lay, values):
+    lanes = lax.broadcasted_iota(jnp.int32, (lay.tokens, lay.inner), 1)
+    spread = values[:, lay.step_lane : lay.step_lane + 1]
+    for j in range(1, lay.heads):
+        own = values[:, lay.step_lane + j : lay.step_lane + j + 1]
+        spread = jnp.where(lanes >= j * lay.hdim, own, spread)
+    return spread
+
+
+def head_lanes(lay, block, j):
+    lanes = lax.broadcasted_iota(jnp.int32, block.shape, 1)
+    kept = (lanes >= j * lay.hdim) & (lanes < (j + 1) * lay.hdim)
+    return jnp.where(kept, block, jnp.zeros_like(block))
+
+
+def head_selector(lay):
+    channel = lax.broadcasted_iota(jnp.int32, (lay.inner, 128), 0)
+    lane = lax.broadcasted_iota(jnp.int32, (lay.inner, 128), 1) - lay.step_lane
+    inside = (channel >= lane * lay.hdim) & (channel < (lane + 1) * lay.hdim)
+    return inside.astype(jnp.float32)
+
+
+def row_sums(values):
+    return lax.dot_general(
+        jnp.ones((8, values.shape[1]), jnp.float32),
+        values,
+        (((1,), (1,)), ((), ())),
+        precision=HIGH,
+        preferred_element_type=jnp.float32,
+    )
+
+
+def mixer_forward(lay, pieces, weights, params, meta, head):
+    count, parts = (len(pieces), len(weights))
+    half = pieces[0].shape[0]
+    chunk = lay.width // parts
+
+    def body(*refs):
+        piece_refs, weight_refs = (refs[:count], refs[count : count + parts])
+        params, meta, head = refs[count + parts : count + parts + 3]
+        (mixer_in, raw, cumul, intra, gated, squares, gains) = refs[count + parts + 3 : -4]
+        hidden, act, stepped, column = refs[-4:]
+        put_pieces(hidden, piece_refs, head[0], half)
+        column[...] = meta[...].T
+        tile = lay.gain // 128 * 128
+        row = lay.gain - tile
+        for k in range(parts):
+            turned = weight_refs[k][:, tile : tile + 128].astype(jnp.float32).T
+            gains[0:8, k * chunk : (k + 1) * chunk] = jnp.concatenate(
+                [turned[row : row + 2], jnp.zeros((6, chunk), jnp.float32)], axis=0
+            )
+
+        def project(at, carry):
+            start = pl.multiple_of(at * ROWS, ROWS)
+            block = hidden[pl.ds(start, ROWS), :].astype(jnp.float32)
+            scale = lax.rsqrt(jnp.mean(block * block, axis=-1, keepdims=True) + EPS)
+            block = (block * scale * gains[0:1, :]).astype(jnp.bfloat16)
+            mixer_in[pl.ds(start, ROWS), :] = block
+            raw[pl.ds(start, ROWS), :] = times_pieces(block, weight_refs)
+            return carry
+
+        lax.fori_loop(0, lay.tokens // ROWS, project, 0)
+        masks = column[...]
+        for at in range(0, lay.gate, 128):
+            _, pre = conv_tile(raw, params, masks, at, lay.taps)
+            act[:, at : at + 128] = pre * sigmoid(pre)
+        tile = slice(lay.step_tile, lay.step_tile + 128)
+        step_pre = raw[:, tile] + params[lay.taps + 3 : lay.taps + 4, tile]
+        step = jnp.maximum(step_pre, 0.0) + jnp.log1p(jnp.exp(-jnp.abs(step_pre)))
+        log_decay = -step * params[lay.taps + 4 : lay.taps + 5, tile]
+        value = act[:, lay.value : lay.value + lay.inner]
+        stepped[...] = (value * over_channels(lay, step)).astype(jnp.bfloat16)
+
+        def sums(at, carry):
+            start = pl.multiple_of(at * ROWS, ROWS)
+            mask = allowed_rows(meta, column, start).astype(jnp.bfloat16)
+            cumul[pl.ds(start, ROWS), :] = exact_mm(mask, log_decay, 1)
+            return carry
+
+        lax.fori_loop(0, lay.tokens // ROWS, sums, 0)
+        cumul_row = cumul[...].T
+        input_b = act[:, : lay.nstate].astype(jnp.bfloat16)
+
+        def mix(at, carry):
+            start = pl.multiple_of(at * ROWS, ROWS)
+            allowed = allowed_rows(meta, column, start)
+            readout = act[pl.ds(start, ROWS), lay.nstate : 2 * lay.nstate].astype(jnp.bfloat16)
+            cross = mm(readout, input_b, 1, 1)
+            own = cumul[pl.ds(start, ROWS), :]
+            total = None
+            for j in range(lay.heads):
+                lane = lay.step_lane + j
+                gap = own[:, lane : lane + 1] - cumul_row[lane : lane + 1, :]
+                mixing = jnp.exp(jnp.where(allowed, gap, NEG_LARGE)) * cross
+                term = mm(mixing.astype(jnp.bfloat16), head_lanes(lay, stepped[...], j), 1, 0)
+                total = term if total is None else total + term
+            intra[pl.ds(start, ROWS), :] = total
+            return carry
+
+        lax.fori_loop(0, lay.tokens // ROWS, mix, 0)
+        skip = params[lay.taps + 1 : lay.taps + 2, lay.value : lay.value + lay.inner]
+        gate = raw[:, lay.gate : lay.gate + lay.inner]
+        out = (intra[...] + skip * value) * (gate * sigmoid(gate))
+        gated[...] = out
+        squares[...] = row_sums(out * out)
+
+    tokens = lay.tokens
+    return local_call(
+        body,
+        (
+            shape_of(tokens, lay.width, jnp.bfloat16),
+            shape_of(tokens, lay.total),
+            shape_of(tokens, 128),
+            shape_of(tokens, lay.inner),
+            shape_of(tokens, lay.inner),
+            shape_of(8, tokens),
+            shape_of(8, lay.width),
+        ),
+        [
+            pltpu.VMEM((tokens, lay.width), jnp.bfloat16),
+            pltpu.VMEM((tokens, lay.gate), jnp.float32),
+            pltpu.VMEM((tokens, lay.inner), jnp.bfloat16),
+            pltpu.VMEM((tokens, 8), jnp.float32),
+        ],
+        (*pieces, *weights, params, meta, head),
+    )
+
+
+def turn_lanes(block, cosine, sine, sign):
+    size = block.shape[1]
+    lanes = lax.broadcasted_iota(jnp.int32, block.shape, 1)
+    first = lanes % HDIM < HDIM // 2
+    ahead = pltpu.roll(block, size - HDIM // 2, 1)
+    behind = pltpu.roll(block, HDIM // 2, 1)
+    return block * cosine + sign * jnp.where(first, -ahead, behind) * sine
+
+
+def attention_forward(lay, raw, meta, cosine, sine):
+    def body(raw, meta, cosine, sine, turned, packed, column):
+        column[...] = meta[...].T
+        rotated = turn_lanes(
+            raw[:, lay.query : lay.query + 2 * lay.kv], cosine[...], sine[...], 1.0
+        )
+        turned[...] = rotated.astype(jnp.bfloat16)
+        keys = turned[:, lay.kv :]
+        values = raw[:, lay.attn_value : lay.attn_value + lay.kv].astype(jnp.bfloat16)
+
+        def rows(at, carry):
+            start = pl.multiple_of(at * ROWS, ROWS)
+            allowed = allowed_rows(meta, column, start)
+            query = turned[pl.ds(start, ROWS), : lay.kv]
+            scores = mm(query, keys, 1, 1) * HDIM ** (-0.5)
+            scores = jnp.where(allowed, scores, NEG_LARGE)
+            peak = jnp.max(scores, axis=-1, keepdims=True)
+            total = jnp.sum(jnp.exp(scores - peak), axis=-1, keepdims=True)
+            log_total = peak + jnp.log(total)
+            probs = jnp.exp(scores - log_total).astype(jnp.bfloat16)
+            out = mm(probs, values, 1, 0)
+            packed[pl.ds(start, ROWS), :] = jnp.concatenate(
+                [out, jnp.broadcast_to(log_total, out.shape)], axis=-1
+            )
+            return carry
+
+        lax.fori_loop(0, lay.tokens // ROWS, rows, 0)
+
+    return local_call(
+        body,
+        (shape_of(lay.tokens, 2 * lay.kv, jnp.bfloat16), shape_of(lay.tokens, 2 * lay.kv)),
+        [pltpu.VMEM((lay.tokens, 8), jnp.float32)],
+        (raw, meta, cosine, sine),
+    )
+
+
+def branch_product(lay, gated, packed, squares, params, weights, head, half):
+    def body(gated, packed, squares, params, head, *rest):
+        weights, (branch_in, sent, mine) = (rest[:-3], rest[-3:])
+        scale = lax.rsqrt(squares[...] / lay.inner_width + EPS).T[:, 0:1]
+        gain = params[lay.taps + 2 : lay.taps + 3, lay.value : lay.value + lay.inner]
+        ssm_in = gated[...] * scale * gain
+        branch_in[...] = jnp.concatenate([ssm_in, packed[:, : lay.kv]], axis=-1).astype(
+            jnp.bfloat16
+        )
+        split_product(branch_in, weights, sent, mine, head[0], half)
+
+    rows = lay.tokens // 2
+    return local_call(
+        body,
+        (
+            shape_of(lay.tokens, lay.inner + lay.kv, jnp.bfloat16),
+            shape_of(rows, lay.width, jnp.bfloat16),
+            shape_of(rows, lay.width),
+        ),
+        [],
+        (gated, packed, squares, params, head, *weights),
+    )
+
+
+def halves_product(left, weights, head, half):
+    def body(left, head, *rest):
+        weights, (sent, mine) = (rest[:-2], rest[-2:])
+        split_product(left, weights, sent, mine, head[0], half)
+
+    rows, width = (left.shape[0] // 2, sum(weight.shape[0] for weight in weights))
+    return local_call(
+        body,
+        (shape_of(rows, width, jnp.bfloat16), shape_of(rows, width)),
+        [],
+        (left, head, *weights),
+    )
+
+
+def add_and_part(mine, got, half):
+    count = mine.shape[0] // half
+
+    def body(mine, got, *parts):
+        for j in range(count):
+            rows = slice(j * half, (j + 1) * half)
+            total = mine[rows, :] + got[rows, :].astype(jnp.float32)
+            parts[j][...] = total.astype(parts[j].dtype)
+
+    width = mine.shape[1]
+    return local_call(
+        body,
+        [shape_of(half, width)] + [shape_of(half, width, jnp.bfloat16)] * (count - 1),
+        [],
+        (mine, got),
+    )
+
+
+def exchange(sent, mine, half):
+    own, *parts = add_and_part(mine, partner(sent), half)
+    return [own] + [to_ahead(part, "seq", j + 1) for j, part in enumerate(parts)]
+
+
+def added(parts):
+    total = parts[0][...]
+    for part in parts[1:]:
+        total = total + part[...].astype(jnp.float32)
+    return total
+
+
+def normed_of(values):
+    scale = lax.rsqrt(jnp.mean(values * values, axis=-1, keepdims=True) + EPS)
+    return (values * scale, scale)
+
+
+def mix_and_norm(parts, resid, gains):
+    count = len(parts)
+
+    def body(*refs):
+        resid, gains, mixed, out = refs[count:]
+        total = resid[...].astype(jnp.float32) + added(refs[:count])
+        mixed[...] = total
+        out[...] = (normed_of(total)[0] * gains[1:2, :]).astype(jnp.bfloat16)
+
+    return local_call(
+        body,
+        (shape_of(*resid.shape), shape_of(*resid.shape, jnp.bfloat16)),
+        [],
+        (*parts, resid, gains),
+    )
+
+
+def norm_pull(parts, values, base, gains, row):
+    count = len(parts)
+
+    def body(*refs):
+        values, base, gains, out, rounded, gain_row = refs[count:]
+        gradient = added(refs[:count])
+        normed, scale = normed_of(values[...].astype(jnp.float32))
+        scaled = gradient * gains[row : row + 1, :]
+        mean = jnp.mean(scaled * normed, axis=-1, keepdims=True)
+        total = base[...].astype(jnp.float32) + scale * (scaled - normed * mean)
+        out[...] = total
+        rounded[...] = total.astype(jnp.bfloat16)
+        sums = jnp.sum(gradient * normed, axis=0, keepdims=True)
+        gain_row[...] = jnp.broadcast_to(sums, gain_row.shape)
+
+    return local_call(
+        body,
+        (
+            shape_of(*values.shape),
+            shape_of(*values.shape, jnp.bfloat16),
+            shape_of(8, values.shape[1]),
+        ),
+        [],
+        (*parts, values, base, gains),
+    )
+
+
+def feed_forward(pieces, up_pieces, weights_ffn, weights_down, head):
+    count, parts = (len(pieces), len(weights_ffn))
+    half, width = pieces[0].shape
+    tokens, units = (half * count, weights_down[0].shape[1])
+
+    def body(*refs):
+        weights_ffn = refs[2 * count : 2 * count + parts]
+        weights_down = refs[2 * count + parts : 2 * count + 2 * parts]
+        head = refs[2 * count + 2 * parts]
+        ffn_in, upstream, hidden_act, gradient, sent, mine = refs[-6:]
+        put_pieces(ffn_in, refs[:count], head[0], half)
+        put_pieces(upstream, refs[count : 2 * count], head[0], half)
+
+        def rows(at, carry):
+            start = pl.multiple_of(at * ROWS, ROWS)
+            both = times_pieces(ffn_in[pl.ds(start, ROWS), :], weights_ffn)
+            gate, upward = (both[:, :units], both[:, units:])
+            sigma = sigmoid(gate)
+            act = gate * sigma
+            hidden_act[pl.ds(start, ROWS), :] = (act * upward).astype(jnp.bfloat16)
+            pulled = times_pieces(upstream[pl.ds(start, ROWS), :], weights_down)
+            gradient[pl.ds(start, ROWS), :] = jnp.concatenate(
+                [pulled * upward * sigma * (1.0 + gate * (1.0 - sigma)), pulled * act], axis=-1
+            ).astype(jnp.bfloat16)
+            return carry
+
+        lax.fori_loop(0, tokens // ROWS, rows, 0)
+        split_product(gradient, weights_ffn, sent, mine, head[0], half)
+
+    return local_call(
+        body,
+        (
+            shape_of(tokens, width, jnp.bfloat16),
+            shape_of(tokens, width, jnp.bfloat16),
+            shape_of(tokens, units, jnp.bfloat16),
+            shape_of(tokens, 2 * units, jnp.bfloat16),
+            shape_of(tokens // 2, width, jnp.bfloat16),
+            shape_of(tokens // 2, width),
+        ),
+        [],
+        (*pieces, *up_pieces, *weights_ffn, *weights_down, head),
+    )
+
+
+def branch_backward(lay, pieces, weights, gated, squares, params, head):
+    count = len(pieces)
+    half = pieces[0].shape[0]
+
+    def body(*refs):
+        gated, squares, params, head = refs[count : count + 4]
+        weights, (branch, gradient, overlap) = (refs[count + 4 : -3], refs[-3:])
+        put_pieces(branch, refs[:count], head[0], half)
+        gradient[...] = times_pieces(branch[...], weights)
+        scale = lax.rsqrt(squares[...] / lay.inner_width + EPS).T[:, 0:1]
+        gain = params[lay.taps + 2 : lay.taps + 3, lay.value : lay.value + lay.inner]
+        overlap[...] = row_sums(gradient[:, : lay.inner] * gain * (gated[...] * scale))
+
+    return local_call(
+        body,
+        (
+            shape_of(lay.tokens, lay.width, jnp.bfloat16),
+            shape_of(lay.tokens, lay.inner + lay.kv),
+            shape_of(8, lay.tokens),
+        ),
+        [],
+        (*pieces, gated, squares, params, head, *weights),
+    )
+
+
+def attention_backward(lay, gradient, raw, turned, packed, meta, cosine, sine):
+    def body(
+        gradient, raw, turned, packed, meta, cosine, sine, grad_turned, grad_values, column, pulls
+    ):
+        column[...] = meta[...].T
+        keys = turned[:, lay.kv :]
+        values = raw[:, lay.attn_value : lay.attn_value + lay.kv].astype(jnp.bfloat16)
+        pulls[...] = jnp.zeros_like(pulls)
+        grad_values[...] = jnp.zeros_like(grad_values)
+
+        def rows(at, carry):
+            start = pl.multiple_of(at * ROWS, ROWS)
+            allowed = allowed_rows(meta, column, start)
+            query = turned[pl.ds(start, ROWS), : lay.kv]
+            saved = packed[pl.ds(start, ROWS), :]
+            pulled = gradient[pl.ds(start, ROWS), lay.inner :]
+            delta = jnp.sum(pulled * saved[:, : lay.kv], axis=-1, keepdims=True)
+            pulled = pulled.astype(jnp.bfloat16)
+            scores = mm(query, keys, 1, 1) * HDIM ** (-0.5)
+            scores = jnp.where(allowed, scores, NEG_LARGE)
+            probs = jnp.exp(scores - saved[:, lay.kv : lay.kv + 1])
+            grad_values[...] += mm(probs.astype(jnp.bfloat16), pulled, 0, 0)
+            grad_probs = mm(pulled, values, 1, 1)
+            grad_scores = (probs * (grad_probs - delta) * HDIM ** (-0.5)).astype(jnp.bfloat16)
+            pulls[pl.ds(start, ROWS), : lay.kv] = mm(grad_scores, keys, 1, 0)
+            pulls[:, lay.kv :] += mm(grad_scores, query, 0, 0)
+            return carry
+
+        lax.fori_loop(0, lay.tokens // ROWS, rows, 0)
+        grad_turned[...] = turn_lanes(pulls[...], cosine[...], sine[...], -1.0)
+
+    return local_call(
+        body,
+        (shape_of(lay.tokens, 2 * lay.kv), shape_of(lay.tokens, lay.kv)),
+        [
+            pltpu.VMEM((lay.tokens, 8), jnp.float32),
+            pltpu.VMEM((lay.tokens, 2 * lay.kv), jnp.float32),
+        ],
+        (gradient, raw, turned, packed, meta, cosine, sine),
+    )
+
+
+def mixer_backward(
+    lay, gradient, raw, cumul, intra, squares, overlap, params, meta, grad_turned, grad_values
+):
+    def body(
+        gradient,
+        raw,
+        cumul,
+        intra,
+        squares,
+        overlap,
+        params,
+        meta,
+        grad_turned,
+        grad_values,
+        grad_raw,
+        small,
+        column,
+        act,
+        stepped,
+        grad_y,
+        grad_act,
+        grad_stepped,
+        grad_step,
+    ):
+        taps, inner = (lay.taps, lay.inner)
+        channels = slice(lay.value, lay.value + inner)
+        column[...] = meta[...].T
+        masks = column[...]
+        small[...] = jnp.zeros_like(small)
+        for at in range(0, lay.gate, 128):
+            _, pre = conv_tile(raw, params, masks, at, taps)
+            act[:, at : at + 128] = pre * sigmoid(pre)
+        tile = slice(lay.step_tile, lay.step_tile + 128)
+        step_pre = raw[:, tile] + params[taps + 3 : taps + 4, tile]
+        step = jnp.maximum(step_pre, 0.0) + jnp.log1p(jnp.exp(-jnp.abs(step_pre)))
+        rate = params[taps + 4 : taps + 5, tile]
+        stepped[...] = (act[:, channels] * over_channels(lay, step)).astype(jnp.bfloat16)
+        scale = lax.rsqrt(squares[...] / lay.inner_width + EPS).T[:, 0:1]
+        shared = (overlap[...] / lay.inner_width).T[:, 0:1]
+        skip = params[taps + 1 : taps + 2, channels]
+        gain = params[taps + 2 : taps + 3, channels]
+        gate = raw[:, lay.gate : lay.gate + inner]
+        gate_sigma = sigmoid(gate)
+        value = act[:, channels]
+        out = intra[...] + skip * value
+        normed = out * gate * gate_sigma * scale
+        pulled = gradient[:, :inner]
+        small[taps + 2 : taps + 3, channels] = jnp.sum(pulled * normed, axis=0, keepdims=True)
+        pulled = scale * (pulled * gain - normed * shared)
+        grad_gate = pulled * out * gate_sigma * (1.0 + gate * (1.0 - gate_sigma))
+        pulled = pulled * gate * gate_sigma
+        small[taps + 1 : taps + 2, channels] = jnp.sum(pulled * value, axis=0, keepdims=True)
+        grad_y[...] = pulled.astype(jnp.bfloat16)
+        grad_act[:, channels] = skip * pulled
+        grad_act[:, : lay.nstate] = jnp.zeros((lay.tokens, lay.nstate), jnp.float32)
+        grad_stepped[...] = jnp.zeros_like(grad_stepped)
+        cumul_row = cumul[...].T
+        input_b = act[:, : lay.nstate].astype(jnp.bfloat16)
+
+        def mix(at, carry):
+            start = pl.multiple_of(at * ROWS, ROWS)
+            rows = pl.ds(start, ROWS)
+            allowed = allowed_rows(meta, column, start)
+            readout = act[rows, lay.nstate : 2 * lay.nstate].astype(jnp.bfloat16)
+            cross = mm(readout, input_b, 1, 1)
+            own = cumul[rows, :]
+            grad_cross, total = (None, None)
+            for j in range(lay.heads):
+                lane = lay.step_lane + j
+                gap = own[:, lane : lane + 1] - cumul_row[lane : lane + 1, :]
+                decay = jnp.exp(jnp.where(allowed, gap, NEG_LARGE))
+                pulled = head_lanes(lay, grad_y[rows, :], j)
+                term = mm((decay * cross).astype(jnp.bfloat16), pulled, 0, 0)
+                total = term if total is None else total + term
+                term = mm(pulled, stepped[...], 1, 1) * decay
+                grad_cross = term if grad_cross is None else grad_cross + term
+            grad_stepped[...] += total
+            grad_cross = grad_cross.astype(jnp.bfloat16)
+            grad_act[rows, lay.nstate : 2 * lay.nstate] = mm(grad_cross, input_b, 1, 0)
+            grad_act[:, : lay.nstate] += mm(grad_cross, readout, 0, 0)
+            return carry
+
+        lax.fori_loop(0, lay.tokens // ROWS, mix, 0)
+        selector = head_selector(lay)
+        moved = grad_stepped[...]
+        change = grad_y[...].astype(jnp.float32) * intra[...] - moved * stepped[...].astype(
+            jnp.float32
+        )
+        grad_cumul = jnp.dot(change, selector, precision=HIGH, preferred_element_type=jnp.float32)
+        value = act[:, channels]
+        grad_step[...] = jnp.zeros_like(grad_step)
+        pieces = []
+        rest = grad_cumul
+        for _ in range(3):
+            pieces.append(rest.astype(jnp.bfloat16))
+            rest = rest - pieces[-1].astype(jnp.float32)
+        for at in range(0, lay.tokens, ROWS):
+            mask = allowed_rows(meta, column, at).astype(jnp.bfloat16)
+            for piece in pieces:
+                grad_step[...] += mm(mask, piece[at : at + ROWS], 0, 0)
+        grad_log_decay = grad_step[...]
+        small[taps + 4 : taps + 5, tile] = jnp.sum(
+            grad_log_decay * (-step * rate), axis=0, keepdims=True
+        )
+        from_value = jnp.dot(
+            moved * value, selector, precision=HIGH, preferred_element_type=jnp.float32
+        )
+        grad_step_raw = (from_value - grad_log_decay * rate) * sigmoid(step_pre)
+        small[taps + 3 : taps + 4, tile] = jnp.sum(grad_step_raw, axis=0, keepdims=True)
+        grad_act[:, channels] += moved * over_channels(lay, step)
+        for at in range(0, lay.gate, 128):
+            cols = slice(at, at + 128)
+            source, pre = conv_tile(raw, params, masks, at, taps)
+            sigma = sigmoid(pre)
+            pulled = grad_act[:, cols] * sigma * (1.0 + pre * (1.0 - sigma))
+            if at + 128 > lay.attn_value:
+                lanes = lax.broadcasted_iota(jnp.int32, pulled.shape, 1) + at
+                pulled = jnp.where(lanes < lay.attn_value, pulled, 0.0)
+            small[taps : taps + 1, cols] = jnp.sum(pulled, axis=0, keepdims=True)
+            total = None
+            for k in range(taps):
+                shift = taps - 1 - k
+                masked = pulled * masks[:, 2 + k : 3 + k]
+                moved = pltpu.roll(source, shift, 0) if shift else source
+                small[k : k + 1, cols] = jnp.sum(masked * moved, axis=0, keepdims=True)
+                term = masked * params[k : k + 1, cols]
+                term = pltpu.roll(term, lay.tokens - shift, 0) if shift else term
+                total = term if total is None else total + term
+            grad_raw[:, cols] = total.astype(jnp.bfloat16)
+        grad_raw[:, lay.attn_value : lay.gate] = grad_values[...].astype(jnp.bfloat16)
+        grad_raw[:, tile] = grad_step_raw.astype(jnp.bfloat16)
+        grad_raw[:, lay.gate : lay.step] = grad_gate.astype(jnp.bfloat16)
+        grad_raw[:, lay.query :] = grad_turned[...].astype(jnp.bfloat16)
+
+    tokens = lay.tokens
+    return local_call(
+        body,
+        (shape_of(tokens, lay.total, jnp.bfloat16), shape_of(16, lay.total)),
+        [
+            pltpu.VMEM((tokens, 8), jnp.float32),
+            pltpu.VMEM((tokens, lay.gate), jnp.float32),
+            pltpu.VMEM((tokens, lay.inner), jnp.bfloat16),
+            pltpu.VMEM((tokens, lay.inner), jnp.bfloat16),
+            pltpu.VMEM((tokens, lay.gate), jnp.float32),
+            pltpu.VMEM((tokens, lay.inner), jnp.float32),
+            pltpu.VMEM((tokens, 128), jnp.float32),
+        ],
+        (
+            gradient,
+            raw,
+            cumul,
+            intra,
+            squares,
+            overlap,
+            params,
+            meta,
+            grad_turned,
+            grad_values,
+        ),
+    )
+
+
+def shift_pairs(count, step):
+    return [(i, (i + step) % count) for i in range(count)]
+
+
+def from_ahead(block, axis, step):
+    count = lax.axis_size(axis)
+    return lax.ppermute(block, axis, shift_pairs(count, -step % count))
+
+
+def to_ahead(block, axis, step):
+    return lax.ppermute(block, axis, shift_pairs(lax.axis_size(axis), step))
+
+
+def partner(block):
+    return to_ahead(block, "head", 1)
+
+
+def wrap_slice(block, start, axis):
+    size = block.shape[axis]
+    return lax.dynamic_slice_in_dim(jnp.concatenate([block, block], axis=axis), start, size, axis)
+
+
+def dot_bf(left, right, dims):
+    return lax.dot_general(left, right, (dims, ((), ())), preferred_element_type=jnp.float32)
+
+
+def after(values, others):
+    return lax.optimization_barrier((values, others))[0]
+
+
+def gather_pieces(half):
+    seqs = lax.axis_size("seq")
+    own = [half] + [from_ahead(half, "seq", j) for j in range(1, seqs)]
+    return own + [partner(piece) for piece in own]
+
+
+def sum_tokens(values):
+    seqs = lax.axis_size("seq")
+    values = values + partner(values)
+    block = values.shape[1] // seqs
+    total = values
+    for j in range(1, seqs):
+        total = total + jnp.roll(from_ahead(values, "seq", j), j * block, axis=1)
+    return total
+
+
+def both_halves(half, head_at):
+    other = partner(half)
+    return jnp.where(
+        head_at == 0,
+        jnp.concatenate([half, other], axis=0),
+        jnp.concatenate([other, half], axis=0),
+    )
+
+
+def dp_pieces(own):
+    return [own] + [from_ahead(own, "dp", k) for k in range(1, lax.axis_size("dp"))]
+
+
+def collect_weight_grad(pairs, seq_at):
+    count, seqs = (lax.axis_size("dp"), lax.axis_size("seq"))
+    chunk = pairs[0][0].shape[1] // count
+    total = None
+    for k in list(range(1, count)) + [0]:
+        part = jnp.concatenate(
+            [
+                dot_bf(activation[:, k * chunk : (k + 1) * chunk], gradient, ((0,), (0,)))
+                for activation, gradient in pairs
+            ],
+            axis=-1,
+        )
+        if k:
+            part = to_ahead(part.astype(jnp.bfloat16), "dp", k).astype(jnp.float32)
+        total = part if total is None else total + part
+    rows = total.astype(jnp.bfloat16).reshape(seqs, chunk // seqs, -1)
+    found = []
+    for j in range(seqs):
+        piece = lax.dynamic_index_in_dim(rows, (seq_at - j) % seqs, 0, keepdims=False)
+        found.append(from_ahead(piece, "seq", j) if j else piece)
+    return wrap_slice(jnp.stack(found), (seqs - seq_at) % seqs, 0).astype(jnp.float32)
+
+
+def laid_out(found, first, width):
+    part = jnp.moveaxis(found[:, :, first : first + width], 0, 1)
+    return part.reshape(part.shape[0], -1)
+
+
+def sum_all(values):
+    for axis in ("dp", "seq"):
+        count = lax.axis_size(axis)
+        step = 1
+        while step < count:
+            values = values + lax.ppermute(values, axis, [(i, i ^ step) for i in range(count)])
+            step *= 2
+    return values
+
+
+def fits_whole_sequences(sizes, args):
+    batch, length, width = args[0].shape
+    dps, seqs, heads = sizes
+    tokens, mheads, inner = (length * seqs, args[12].shape[0], args[4].shape[1])
+    attn, kv, bc, units = (args[i].shape[1] for i in (17, 18, 6, 22))
+    powers = all(size & (size - 1) == 0 for size in sizes)
+    even = all(part % seqs == 0 for part in (mheads, inner, attn, units))
+    if not (powers and even and heads == 2 and batch == 1 and tokens <= 1024):
+        return False
+    conv = bc + inner // seqs
+    aligned = bc % 256 == 0 and (conv + kv) % 128 == 0 and (2 * kv) % 128 == 0
+    blocks = tokens % ROWS == 0 and length % 32 == 0 and width % (128 * dps) == 0
+    single = kv == HDIM and attn // seqs == HDIM
+    lane = (conv + kv + inner // seqs) % 128 + mheads // seqs + 2
+    return aligned and blocks and single and units % (128 * seqs) == 0 and lane <= 128
+
+
+def whole_sequences(
+    hidden_in,
+    out_grad,
+    doc_ids,
+    mixer_gain,
+    ssm_gate_proj,
+    ssm_value_proj,
+    ssm_bc_proj,
+    ssm_step_proj,
+    conv_value_kernel,
+    conv_value_bias,
+    conv_bc_kernel,
+    conv_bc_bias,
+    decay_log,
+    step_bias,
+    skip_gain,
+    ssm_norm_gain,
+    ssm_out_proj,
+    query_proj,
+    key_proj,
+    value_proj,
+    attn_out_proj,
+    ffn_gain,
+    ffn_gate_proj,
+    ffn_up_proj,
+    ffn_down_proj,
+):
+    bf16, f32 = (jnp.bfloat16, jnp.float32)
+    dps, seqs, heads = (lax.axis_size(axis) for axis in ("dp", "seq", "head"))
+    dp_at, seq_at, head_at = (lax.axis_index(axis) for axis in ("dp", "seq", "head"))
+    _, length, width = hidden_in.shape
+    tokens = length * seqs
+    half = length // heads
+    rows = ssm_gate_proj.shape[0]
+    chunk = width // dps
+    inner = ssm_gate_proj.shape[1] // seqs
+    mheads = decay_log.shape[0] // seqs
+    kv = key_proj.shape[1]
+    bc = ssm_bc_proj.shape[1]
+    units = ffn_gate_proj.shape[1] // seqs
+    taps = conv_value_kernel.shape[0]
+    lay = Layout(
+        tokens, width, inner, bc // 2, kv, mheads, taps, inner * seqs * heads
+    )
+    head = jnp.reshape(head_at, (1,)).astype(jnp.int32)
+
+    def rotated(block):
+        return wrap_slice(block, dp_at * chunk, block.ndim - 1)
+
+    def unrotated(block):
+        return wrap_slice(block, (dps - dp_at) % dps * chunk, block.ndim - 1)
+
+    def cut(block):
+        return jnp.moveaxis(block.reshape(rows, seqs, -1), 1, 0)
+
+    def same(block):
+        return jnp.broadcast_to(block[None], (seqs,) + block.shape)
+
+    def own_part(block):
+        size = block.shape[-1] // seqs
+        return lax.dynamic_slice_in_dim(block, seq_at * size, size, block.ndim - 1)
+
+    def exchanged_rows(pieces):
+        found = lax.all_to_all(pieces, "seq", 0, 0, tiled=True)
+        return found.reshape(-1, found.shape[-1])
+
+    first_rows = exchanged_rows(
+        jnp.concatenate(
+            [
+                same(ssm_bc_proj),
+                cut(ssm_value_proj),
+                same(value_proj),
+                cut(ssm_gate_proj),
+                cut(ssm_step_proj),
+                same(mixer_gain[:, None]),
+                same(ffn_gain[:, None]),
+                jnp.zeros((seqs, rows, lay.query - lay.gain - 2), bf16),
+                cut(query_proj),
+                same(key_proj),
+            ],
+            axis=-1,
+        )
+    )
+    hidden_half = rotated(lax.dynamic_slice_in_dim(hidden_in[0], head_at * half, half, 0))
+    hidden = gather_pieces(hidden_half)
+    weight_in = dp_pieces(first_rows)
+    second_rows = exchanged_rows(
+        after(
+            jnp.concatenate(
+                [
+                    cut(ffn_gate_proj),
+                    cut(ffn_up_proj),
+                    cut(ssm_out_proj.T),
+                    cut(attn_out_proj.T),
+                    cut(ffn_down_proj.T),
+                ],
+                axis=-1,
+            ),
+            first_rows,
+        )
+    )
+    grad_half = after(
+        rotated(lax.dynamic_slice_in_dim(out_grad[0], head_at * half, half, 0)), first_rows
+    )
+    upstream_pieces = gather_pieces(grad_half)
+    weight_rest = dp_pieces(second_rows)
+    branch_width = inner + kv
+    weight_ffn = [window(piece, 0, 2 * units) for piece in weight_rest]
+    weight_out = [window(piece, 2 * units, branch_width) for piece in weight_rest]
+    weight_down = [window(piece, 2 * units + branch_width, units) for piece in weight_rest]
+
+    order = jnp.arange(tokens, dtype=jnp.int32)
+    positions = (order + seq_at * length) % tokens
+    docs = wrap_slice(doc_ids[0], seq_at * length, 0)
+    meta = [positions, docs]
+    for k in range(taps):
+        shift = taps - 1 - k
+        meta.append((positions >= shift) & (jnp.roll(docs, shift) == docs))
+    meta = jnp.stack([row.astype(f32) for row in meta] + [jnp.zeros((tokens,), f32)] * (6 - taps))
+    cosine, sine = rope_tables(positions, HDIM)
+    cosine = jnp.tile(cosine, (1, 2 * 2 * kv // HDIM))
+    sine = jnp.tile(sine, (1, 2 * 2 * kv // HDIM))
+
+    def placed_row(values, first):
+        return jnp.pad(values, ((0, 0), (first, lay.total - first - values.shape[1])))
+
+    params = jnp.concatenate(
+        [
+            placed_row(
+                jnp.concatenate(
+                    [
+                        jnp.concatenate([conv_bc_kernel, own_part(conv_value_kernel)], axis=-1),
+                        jnp.concatenate([conv_bc_bias, own_part(conv_value_bias)])[None],
+                    ],
+                    axis=0,
+                ),
+                0,
+            ),
+            placed_row(
+                jnp.stack(
+                    [jnp.repeat(own_part(skip_gain), lay.hdim), own_part(ssm_norm_gain)]
+                ),
+                lay.value,
+            ),
+            placed_row(
+                jnp.stack([own_part(step_bias), jnp.exp(own_part(decay_log))]), lay.step
+            ),
+            jnp.zeros((11 - taps, lay.total), f32),
+        ],
+        axis=0,
+    )
+
+    mixer_in, raw, cumul, intra, gated, squares, gains = mixer_forward(
+        lay, hidden, weight_in, params, meta, head
+    )
+    squares = sum_tokens(squares)
+    turned, packed = attention_forward(lay, raw, meta, cosine, sine)
+    branch_in, sent, mine = branch_product(
+        lay, gated, packed, squares, params, weight_out, head, half
+    )
+    mixed, ffn_half = mix_and_norm(exchange(sent, mine, half), hidden_half, gains)
+    ffn_in, upstream, hidden_act, grad_ffn, sent, mine = feed_forward(
+        gather_pieces(ffn_half), upstream_pieces, weight_ffn, weight_down, head
+    )
+    parts = exchange(sent, mine, half)
+    grad_mixed, branch_half, grad_ffn_gain = norm_pull(parts, mixed, grad_half, gains, 1)
+    branch, grad_branch, overlap = branch_backward(
+        lay, gather_pieces(branch_half), weight_out, gated, squares, params, head
+    )
+    overlap = sum_tokens(overlap)
+    found_ffn = collect_weight_grad(
+        after([(ffn_in, grad_ffn), (upstream, hidden_act)], parts[0]), seq_at
+    )
+    found_branch = collect_weight_grad([(branch, branch_in)], seq_at)
+    grad_turned, grad_values = attention_backward(
+        lay, grad_branch, raw, turned, packed, meta, cosine, sine
+    )
+    sent, mine = halves_product(after(hidden_act, grad_branch), weight_down, head, half)
+    block_half = sum(
+        part.astype(f32) for part in exchange(sent, mine, half)
+    )
+    block_half = (mixed + block_half).astype(bf16)
+    block_out = unrotated(both_halves(block_half, head_at))[None]
+
+    grad_raw, small = mixer_backward(
+        lay,
+        grad_branch,
+        raw,
+        cumul,
+        intra,
+        squares,
+        overlap,
+        params,
+        meta,
+        grad_turned,
+        grad_values,
+    )
+    sent, mine = halves_product(grad_raw, weight_in, head, half)
+    hidden_grad, _, grad_mixer_gain = norm_pull(
+        exchange(sent, mine, half), hidden_half, grad_mixed, gains, 0
+    )
+    hidden_grad = unrotated(both_halves(hidden_grad, head_at))[None]
+    found_in = collect_weight_grad([(mixer_in, grad_raw)], seq_at)
+
+    def in_place(block):
+        size = block.shape[1]
+        return lax.dynamic_update_slice_in_dim(
+            jnp.zeros((block.shape[0], size * seqs), f32), block, seq_at * size, 1
+        )
+
+    channel = in_place(small[: taps + 3, lay.value : lay.value + inner])
+    per_head = in_place(small[taps + 3 : taps + 5, lay.step : lay.step + mheads])
+    whole = small[: taps + 1, :bc]
+    grad_gains = unrotated(jnp.concatenate([grad_mixer_gain[:1], grad_ffn_gain[:1]], axis=0))
+    listed = [channel, per_head, whole, grad_gains]
+    summed = sum_all(jnp.concatenate([part.reshape(-1) for part in listed]))
+    at_whole = channel.size + per_head.size
+    shared = summed[at_whole:]
+    shared = shared + partner(shared)
+    channel = summed[: channel.size].reshape(channel.shape)
+    per_head = summed[channel.size : at_whole].reshape(per_head.shape)
+    whole = shared[: whole.size].reshape(whole.shape)
+    grad_gains = lax.dynamic_slice_in_dim(
+        shared[whole.size :].reshape(grad_gains.shape), (dp_at * seqs + seq_at) * rows, rows, 1
+    )
+    over_seq = jnp.sum(found_in, axis=0)
+    grad_bc_proj = over_seq[:, :bc]
+    grad_bc_proj = grad_bc_proj + partner(grad_bc_proj)
+    return (
+        block_out,
+        hidden_grad,
+        grad_gains[0],
+        laid_out(found_in, lay.gate, inner),
+        laid_out(found_in, lay.value, inner),
+        grad_bc_proj,
+        laid_out(found_in, lay.step, mheads),
+        channel[:taps],
+        channel[taps],
+        whole[:taps],
+        whole[taps],
+        per_head[1],
+        per_head[0],
+        jnp.sum(channel[taps + 1].reshape(-1, lay.hdim), axis=-1),
+        channel[taps + 2],
+        laid_out(found_branch, 0, inner).T,
+        laid_out(found_in, lay.query, kv),
+        over_seq[:, lay.query + kv :],
+        over_seq[:, lay.attn_value : lay.gate],
+        laid_out(found_branch, inner, kv).T,
+        grad_gains[1],
+        laid_out(found_ffn, 0, units),
+        laid_out(found_ffn, units, units),
+        laid_out(found_ffn, 2 * units, units).T,
+    )
+
+
+def block_step(*args):
+    sizes = tuple(lax.axis_size(axis) for axis in ("dp", "seq", "head"))
+    if fits_whole_sequences(sizes, args):
+        return whole_sequences(*args)
+    return local(*args)
+
+
 def solution(mesh):
     placed = (
         P("dp", "seq", None),
@@ -632,7 +1705,7 @@
         P("head", ("dp", "seq")),
     )
     return jax.shard_map(
-        local,
+        block_step,
         mesh=mesh,
         in_specs=placed,
         out_specs=(

time: 1930 us -> 367 us (0.19)
  waiting for transfers between devices: 1320 us -> 122 us
  blocking collectives: 391 us -> 0 us
  starting transfers between devices: 12.2 us -> 95.6 us
  Pallas kernels: 0 us -> 70 us
  matrix products: 86.1 us -> 21.4 us
  other arithmetic: 51.9 us -> 9.97 us
    reduce_scatter x12 -> x0, waiting for transfers between devices: 1010 us -> none  [the longest x1 137 us: local(): lax.psum_scatter(weight_grad(mixer_in, grad_gate_in), ('dp', 'seq'), scat...]
    all_gather x8 -> x0, blocking collectives: 269 us -> none  [the longest x1 46 us: local(): lax.all_gather(query_proj, ('dp', 'seq'), axis=0, tiled=True)]
    all_gather x8 -> x0, waiting for transfers between devices: 208 us -> none  [the longest x1 62.6 us: local(): lax.all_gather(ffn_gate_proj, ('dp', 'seq'), axis=0, tiled=True)]
    unnamed x2 -> x0, blocking collectives: 117 us -> none
    ppermute x4 -> x84, waiting for transfers between devices: 4.65 us -> 115 us  [the longest x33 78.8 us: from_ahead(): return lax.ppermute(block, axis, shift_pairs(count, -step % count))]
    ppermute x4 -> x84, starting transfers between devices: 10.6 us -> 88.1 us  [the longest x33 42.8 us: from_ahead(): return lax.ppermute(block, axis, shift_pairs(count, -step % count))]
    pallas_call x0 -> x16, Pallas kernels: none -> 70 us  [local_call(): pl.pallas_call(body, out_shape=out_shape, in_specs=[spec(arg) for arg in...]
    dot_general x54 -> x16, matrix products: 84.9 us -> 21.4 us  [dot_bf(): lax.dot_general(left, right, (dims, ((), ())), preferred_element_type=jnp...]
  transfers between devices with their start and end apart: 28 -> 86, of which waited for: 20 -> 29; matrix products, arithmetic and copies ran while one was open for 6% -> 17% of each run, Pallas kernels for 0% -> 16%
where the time goes in v2:
time: 367 us; the launch traced here: 365 us
  waiting for transfers between devices  122 us (33%)
  starting transfers between devices  95.6 us (26%)
  Pallas kernels  70 us (19%)
  local copies, waits for them, and re-layouts  43.7 us (12%)
  matrix products  21.4 us (6%)
  other arithmetic  9.97 us (3%)
    ppermute x33, waiting for transfers between devices, from_ahead(): return lax.ppermute(block, axis, shift_pairs(count, -step % count))  78.8 us
    pallas_call x16, Pallas kernels, local_call(): pl.pallas_call(body, out_shape=out_shape, in_specs=[spec(arg) for arg in...  70 us
    ppermute x33, starting transfers between devices, from_ahead(): return lax.ppermute(block, axis, shift_pairs(count, -step % count))  42.8 us
    ppermute x47, starting transfers between devices, to_ahead(): return lax.ppermute(block, axis, shift_pairs(lax.axis_size(axis), step))  37.2 us
    ppermute x47, waiting for transfers between devices, to_ahead(): return lax.ppermute(block, axis, shift_pairs(lax.axis_size(axis), step))  29 us
    dot_general x16, matrix products, dot_bf(): lax.dot_general(left, right, (dims, ((), ())), preferred_element_type=jnp...  21.4 us
    unnamed x195, local copies, waits for them, and re-layouts  11.7 us
    ppermute x4, starting transfers between devices, sum_all(): lax.ppermute(values, axis, [(i, i ^ step) for i in range(count)])  8.04 us
  transfers between devices with their start and end apart: 86, of which 29 were waited for; matrix products, arithmetic and copies ran while one was open for 17% of the time, Pallas kernels for 16%

profile of v2, /device:TPU:0, one launch (start us, length us, event | category | flops | bytes accessed | tf_op | source)
XLA Modules:
  0.0 365.3 jit_solution(9003586056998456534)
XLA Ops:
  1.7 5.1 %collective-permute-start = (bf16[64,1024]{1,0:T(8,128)(2,1)S(1)}, bf16[64,1024]{1,0:T(8,128)(2,1)S(1)}, u32[]{:S(2)}, u32[]{:S(2)}) collective-permute-start(bf16[64,1024]{1,0:T(8,128)(2,1)S(1)} %fusion.29.refs_0_.refs_4_), channel_id=1, source_target_pairs={{0,6},{2,0},{4,2},{6,4},{1,7},{3,1},{5,3},{7,5},{8,14},{10,8},{12,... | collective-permute-start | bytes 393224 | tf_op jit(solution)/shard_map/ppermute | solution.py:1308
  13.3 4.1 %all-to-all-start = ((bf16[4,64,896]{2,1,0:T(8,128)(2,1)}), bf16[4,64,896]{2,1,0:T(8,128)(2,1)S(1)}, u32[]{:S(2)}, u32[]{:S(2)}) async-start(bf16[4,64,896]{2,1,0:T(8,128)(2,1)} %concatenate.115), calls=%async_computation | async-start | bytes 917504 | tf_op jit(solution)/shard_map/all_to_all | solution.py:1479
  22.3 7.6 %all-to-all-done = bf16[4,64,896]{2,1,0:T(8,128)(2,1)S(1)} async-done(((bf16[4,64,896]{2,1,0:T(8,128)(2,1)}), bf16[4,64,896]{2,1,0:T(8,128)(2,1)S(1)}, u32[]{:S(2)}, u32[]{:S(2)}) %all-to-all-start) | async-done | bytes 458784 | tf_op jit(solution)/shard_map/all_to_all | solution.py:1479
  32.8 3.5 all-to-all-start.1
  43.3 10.1 %collective-permute-done.8.refs_10_.rest_2_ = bf16[256,896]{1,0:T(8,128)(2,1)S(1)} collective-permute-done((bf16[256,896]{1,0:T(8,128)(2,1)S(1)}, bf16[256,896]{1,0:T(8,128)(2,1)S(1)}, u32[]{:S(2)}, u32[]{:S(2)}) %collective-permute-start.8) | collective-permute-done | bytes 458784 | tf_op jit(solution)/shard_map/ppermute | solution.py:1308
  54.3 10.4 %shard_map.424 = (bf16[512,1024]{1,0:T(8,128)(2,1)}, f32[512,896]{1,0:T(8,128)}, f32[512,128]{1,0:T(8,128)}, f32[512,192]{1,0:T(8,128)}, f32[512,192]{1,0:T(8,12...) custom-call(bf16[64,1024]{1,0:T(8,128)(2,1)} %copy-done.8, bf16[64,1024]{1,0:T(8,128)(2,1)} %copy-done.23, ...), custom_call_target="tpu_custom_call" | custom-call | tf_op jit(solution)/shard_map/pallas_call | solution.py:647
  73.5 5.1 %shard_map.425 = (bf16[512,128]{1,0:T(8,128)(2,1)}, f32[512,128]{1,0:T(8,128)}) custom-call(f32[512,896]{1,0:T(8,128)} %get-tuple-element.84.raw, f32[8,512]{1,0:T(8,128)} %stack.90.refs_13_.meta, f32[512,128]{1,0:T(8,128)} %copy.136.cosine, f32[512,128]{1,0:T(8,128)} %copy.137.sine), custom_call_target="tpu_custom_call" | custom-call | tf_op jit(solution)/shard_map/pallas_call | solution.py:647
  79.2 4.5 %collective-permute-done.14.rest_1_.refs_17_.refs_21_.refs_13_ = bf16[256,1024]{1,0:T(8,128)(2,1)S(1)} collective-permute-done((bf16[256,1024]{1,0:T(8,128)(2,1)S(1)}, bf16[256,1024]{1,0:T(8,128)(2,1)S(1)}, u32[]{:S(2)}, u32[]{:S(2)}) %collective-permute-start.14) | collective-permute-done | bytes 524320 | tf_op jit(solution)/shard_map/ppermute | solution.py:1308
  83.7 10.1 %collective-permute-done.15.rest_2_.refs_18_.refs_22_.refs_14_ = bf16[256,1024]{1,0:T(8,128)(2,1)S(1)} collective-permute-done((bf16[256,1024]{1,0:T(8,128)(2,1)S(1)}, bf16[256,1024]{1,0:T(8,128)(2,1)S(1)}, u32[]{:S(2)}, u32[]{:S(2)}) %collective-permute-start.15) | collective-permute-done | bytes 524320 | tf_op jit(solution)/shard_map/ppermute | solution.py:1308
  94.8 3.2 shard_map.426
  98.2 3.3 collective-permute-start.28
  107.4 2.9 collective-permute-start.20
  110.3 8.1 %collective-permute-done.29.refs_10_ = bf16[64,1024]{1,0:T(8,128)(2,1)S(1)} collective-permute-done((bf16[64,1024]{1,0:T(8,128)(2,1)S(1)}, bf16[64,1024]{1,0:T(8,128)(2,1)S(1)}, u32[]{:S(2)}, u32[]{:S(2)}) %collective-permute-start.29) | collective-permute-done | bytes 131104 | tf_op jit(solution)/shard_map/ppermute | solution.py:1308
  118.9 4.5 %collective-permute-done.19.refs_2_ = bf16[64,1024]{1,0:T(8,128)(2,1)S(1)} collective-permute-done((bf16[64,1024]{1,0:T(8,128)(2,1)}, bf16[64,1024]{1,0:T(8,128)(2,1)S(1)}, u32[]{:S(2)}, u32[]{:S(2)}) %collective-permute-start.19) | collective-permute-done | bytes 131104 | tf_op jit(solution)/shard_map/ppermute | solution.py:1312
  133.2 9.0 %collective-permute-done.22.refs_2_ = bf16[64,1024]{1,0:T(8,128)(2,1)S(1)} collective-permute-done((bf16[64,1024]{1,0:T(8,128)(2,1)}, bf16[64,1024]{1,0:T(8,128)(2,1)S(1)}, u32[]{:S(2)}, u32[]{:S(2)}) %collective-permute-start.22) | collective-permute-done | bytes 131104 | tf_op jit(solution)/shard_map/ppermute | solution.py:1308
  144.8 6.4 %shard_map.429 = (bf16[512,1024]{1,0:T(8,128)(2,1)}, bf16[512,1024]{1,0:T(8,128)(2,1)}, bf16[512,256]{1,0:T(8,128)(2,1)}, bf16[512,512]{1,0:T(8,128)(2,1)}, bf16...) custom-call(bf16[64,1024]{1,0:T(8,128)(2,1)} %get-tuple-element.96.refs_0_, bf16[64,1024]{1,0:T(8,128)(2,1)} %copy-done.33, ...), custom_call_target="tpu_custom_call" | custom-call | tf_op jit(solution)/shard_map/pallas_call | solution.py:647
  162.5 3.0 collective-permute-start.38
  166.4 3.4 collective-permute-done.36.refs_1_
  169.8 4.6 %collective-permute-done.37.refs_2_ = bf16[64,1024]{1,0:T(8,128)(2,1)S(1)} collective-permute-done((bf16[64,1024]{1,0:T(8,128)(2,1)S(1)}, bf16[64,1024]{1,0:T(8,128)(2,1)S(1)}, u32[]{:S(2)}, u32[]{:S(2)}) %collective-permute-start.37) | collective-permute-done | bytes 131104 | tf_op jit(solution)/shard_map/ppermute | solution.py:1312
  184.1 8.3 %collective-permute-done.40.refs_2_ = bf16[64,1024]{1,0:T(8,128)(2,1)S(1)} collective-permute-done((bf16[64,1024]{1,0:T(8,128)(2,1)}, bf16[64,1024]{1,0:T(8,128)(2,1)S(1)}, u32[]{:S(2)}, u32[]{:S(2)}) %collective-permute-start.40) | collective-permute-done | bytes 131104 | tf_op jit(solution)/shard_map/ppermute | solution.py:1308
  198.5 3.7 %shard_map.432 = (bf16[512,1024]{1,0:T(8,128)(2,1)}, f32[512,256]{1,0:T(8,128)}, f32[8,512]{1,0:T(8,128)}) custom-call(bf16[64,1024]{1,0:T(8,128)(2,1)} %get-tuple-element.105.refs_0_, bf16[64,1024]{1,0:T(8,128)(2,1)} %copy-done.37, bf16[64,1024]{1,0:T(8,128)(2,1)} %copy-done.40, bf16[64,1024]{1,0:T(8,128)(2,1)} %copy-done.41, ...), custom_call_target="tpu_custom_call" | custom-call | tf_op jit(solution)/shard_map/pallas_call | solution.py:647
  215.0 6.0 %shard_map.435 = (f32[512,128]{1,0:T(8,128)}, f32[512,64]{1,0:T(8,128)}) custom-call(f32[512,256]{1,0:T(8,128)} %get-tuple-element.106.gradient, f32[512,896]{1,0:T(8,128)} %get-tuple-element.84.raw, bf16[512,128]{1,0:T(8,128)(2,1)} %get-tuple-element.117.turned, f32[512,128]{1,0:T(8,128)} %get-tuple-element.85.packed, f32[8,512]{1,0:T(8,128)} %stack.90.refs_13_.meta, ...), custom_call_target="tpu_custom_call" | custom-call | tf_op jit(solution)/shard_map/pallas_call | solution.py:647
  221.0 2.8 shard_map.433
  225.0 9.7 %collective-permute-start.72 = (bf16[256,256]{1,0:T(8,128)(2,1)}, bf16[256,256]{1,0:T(8,128)(2,1)}, u32[]{:S(2)}, u32[]{:S(2)}) collective-permute-start(bf16[256,256]{1,0:T(8,128)(2,1)} %convolution_convert_fusion.11), channel_id=1, source_target_pairs={{0,8},{8,16},{16,24},{24,0},{1,9},{9,17},{17,25},{25,1},{2,10},{10... | collective-permute-start | bytes 393224 | tf_op jit(solution)/shard_map/ppermute | solution.py:1312
  236.4 13.0 %shard_map.436 = (bf16[512,896]{1,0:T(8,128)(2,1)}, f32[16,896]{1,0:T(8,128)}) custom-call(f32[512,256]{1,0:T(8,128)} %get-tuple-element.106.gradient, f32[512,896]{1,0:T(8,128)} %get-tuple-element.84.raw, f32[512,128]{1,0:T(8,128)} %get-tuple-element.114.cumul, f32[512,192]{1,0:T(8,128)} %get-tuple-element.115.intra, f32[8,512]{1,0:T(8,128)} %fusion.31.squares.refs_9_, ...), custom_call_target="tpu_custom_call" | custom-call | tf_op jit(solution)/shard_map/pallas_call | solution.py:647
  258.9 4.2 %shard_map.437 = (bf16[256,1024]{1,0:T(8,128)(2,1)}, f32[256,1024]{1,0:T(8,128)}) custom-call(bf16[512,896]{1,0:T(8,128)(2,1)} %get-tuple-element.120.left, s32[1]{0:T(128)} %bitcast.15.refs_14_.head.refs_24_.refs_11_, bf16[256,896]{1,0:T(8,128)(2,1)} %bitcast.178, bf16[256,896]{1,0:T(8,128)(2,1)} %copy-done.9, bf16[256,896]{1,0:T(8,128)(2,1)} %copy-done.10, ...), custom_call_target="tpu_custom_call" | custom-call | tf_op jit(solution)/shard_map/pallas_call | solution.py:647
  276.6 3.7 %collective-permute-done.76 = bf16[64,256]{1,0:T(8,128)(2,1)S(1)} collective-permute-done((bf16[64,256]{1,0:T(8,128)(2,1)S(1)}, bf16[64,256]{1,0:T(8,128)(2,1)S(1)}, u32[]{:S(2)}, u32[]{:S(2)}) %collective-permute-start.76) | collective-permute-done | bytes 32800 | tf_op jit(solution)/shard_map/ppermute | solution.py:1308
  281.6 4.4 %collective-permute-done.77 = bf16[64,256]{1,0:T(8,128)(2,1)S(1)} collective-permute-done((bf16[64,256]{1,0:T(8,128)(2,1)S(1)}, bf16[64,256]{1,0:T(8,128)(2,1)S(1)}, u32[]{:S(2)}, u32[]{:S(2)}) %collective-permute-start.77) | collective-permute-done | bytes 32800 | tf_op jit(solution)/shard_map/ppermute | solution.py:1308
  306.6 15.3 %collective-permute-done.69 = bf16[64,896]{0,1:T(8,128)(2,1)S(1)} collective-permute-done((bf16[64,896]{0,1:T(8,128)(2,1)}, bf16[64,896]{0,1:T(8,128)(2,1)S(1)}, u32[]{:S(2)}, u32[]{:S(2)}) %collective-permute-start.69) | collective-permute-done | bytes 114720 | tf_op jit(solution)/shard_map/ppermute | solution.py:1308
  323.1 5.8 %collective-permute-done.56.refs_1_ = bf16[64,1024]{1,0:T(8,128)(2,1)S(1)} collective-permute-done((bf16[64,1024]{1,0:T(8,128)(2,1)}, bf16[64,1024]{1,0:T(8,128)(2,1)S(1)}, u32[]{:S(2)}, u32[]{:S(2)}) %collective-permute-start.56) | collective-permute-done | bytes 131104 | tf_op jit(solution)/shard_map/ppermute | solution.py:1312
  334.6 3.7 %collective-permute-done.58.refs_3_ = bf16[64,1024]{1,0:T(8,128)(2,1)S(1)} collective-permute-done((bf16[64,1024]{1,0:T(8,128)(2,1)S(1)}, bf16[64,1024]{1,0:T(8,128)(2,1)S(1)}, u32[]{:S(2)}, u32[]{:S(2)}) %collective-permute-start.58) | collective-permute-done | bytes 131104 | tf_op jit(solution)/shard_map/ppermute | solution.py:1312
  354.5 3.5 collective-permute-start.63
  (511 shorter events, 170.3 us)
Async XLA Ops:
  1.7 34.6 %collective-permute-start = (bf16[64,1024]{1,0:T(8,128)(2,1)S(1)}, bf16[64,1024]{1,0:T(8,128)(2,1)S(1)}, u32[]{:S(2)}, u32[]{:S(2)}) collective-permute-start(bf16[64,1024]{1,0:T(8,128)(2,1)S(1)} %fusion.29.refs_0_.refs_4_), channel_id=1, source_target_pairs={{0,6},{2,0},{4,2},{6,4},{1,7},{3,1},{5,3},{7,5},{8,14},{10,8},{12,... | collective-permute-start | bytes 393224 | tf_op jit(solution)/shard_map/ppermute | solution.py:1308
  6.9 30.9 %collective-permute-start.1 = (bf16[64,1024]{1,0:T(8,128)(2,1)S(1)}, bf16[64,1024]{1,0:T(8,128)(2,1)S(1)}, u32[]{:S(2)}, u32[]{:S(2)}) collective-permute-start(bf16[64,1024]{1,0:T(8,128)(2,1)S(1)} %fusion.29.refs_0_.refs_4_), channel_id=1, source_target_pairs={{0,4},{2,6},{4,0},{6,2},{1,5},{3,7},{5,1},{7,3},{8,12},{10,14},{12... | collective-permute-start | bytes 393224 | tf_op jit(solution)/shard_map/ppermute | solution.py:1308
  6.9 31.0 %collective-permute-start.2 = (bf16[64,1024]{1,0:T(8,128)(2,1)S(1)}, bf16[64,1024]{1,0:T(8,128)(2,1)S(1)}, u32[]{:S(2)}, u32[]{:S(2)}) collective-permute-start(bf16[64,1024]{1,0:T(8,128)(2,1)S(1)} %fusion.29.refs_0_.refs_4_), channel_id=1, source_target_pairs={{0,2},{2,4},{4,6},{6,0},{1,3},{3,5},{5,7},{7,1},{8,10},{10,12},{12... | collective-permute-start | bytes 393224 | tf_op jit(solution)/shard_map/ppermute | solution.py:1308
  13.3 16.6 %all-to-all-start = ((bf16[4,64,896]{2,1,0:T(8,128)(2,1)}), bf16[4,64,896]{2,1,0:T(8,128)(2,1)S(1)}, u32[]{:S(2)}, u32[]{:S(2)}) async-start(bf16[4,64,896]{2,1,0:T(8,128)(2,1)} %concatenate.115), calls=%async_computation | async-start | bytes 917504 | tf_op jit(solution)/shard_map/all_to_all | solution.py:1479
  32.3 21.1 %collective-permute-start.8 = (bf16[256,896]{1,0:T(8,128)(2,1)S(1)}, bf16[256,896]{1,0:T(8,128)(2,1)S(1)}, u32[]{:S(2)}, u32[]{:S(2)}) collective-permute-start(bf16[256,896]{1,0:T(8,128)(2,1)S(1)} %bitcast.175), channel_id=1, source_target_pairs={{0,16},{8,24},{16,0},{24,8},{1,17},{9,25},{17,1},{25,9},{2,18},{10... | collective-permute-start | bytes 1376264 | tf_op jit(solution)/shard_map/ppermute | solution.py:1308
  32.8 36.1 %all-to-all-start.1 = ((bf16[4,64,1024]{2,1,0:T(8,128)(2,1)}), bf16[4,64,1024]{2,1,0:T(8,128)(2,1)S(1)}, u32[]{:S(2)}, u32[]{:S(2)}) async-start(bf16[4,64,1024]{2,1,0:T(8,128)(2,1)} %concatenate.127), calls=%async_computation.1 | async-start | bytes 1048576 | tf_op jit(solution)/shard_map/all_to_all | solution.py:1479
  36.3 17.1 %collective-permute-start.9 = (bf16[256,896]{1,0:T(8,128)(2,1)S(1)}, bf16[256,896]{1,0:T(8,128)(2,1)S(1)}, u32[]{:S(2)}, u32[]{:S(2)}) collective-permute-start(bf16[256,896]{1,0:T(8,128)(2,1)S(1)} %bitcast.176), channel_id=1, source_target_pairs={{0,8},{8,16},{16,24},{24,0},{1,9},{9,17},{17,25},{25,1},{2,10},{10... | collective-permute-start | bytes 1376264 | tf_op jit(solution)/shard_map/ppermute | solution.py:1308
  69.5 24.4 %collective-permute-start.15 = (bf16[256,1024]{1,0:T(8,128)(2,1)S(1)}, bf16[256,1024]{1,0:T(8,128)(2,1)S(1)}, u32[]{:S(2)}, u32[]{:S(2)}) collective-permute-start(bf16[256,1024]{1,0:T(8,128)(2,1)S(1)} %bitcast.167), channel_id=1, source_target_pairs={{0,16},{8,24},{16,0},{24,8},{1,17},{9,25},{17,1},{25,9},{2,18},{10... | collective-permute-start | bytes 1572872 | tf_op jit(solution)/shard_map/ppermute | solution.py:1308
  70.6 23.3 %collective-permute-start.16 = (bf16[256,1024]{1,0:T(8,128)(2,1)S(1)}, bf16[256,1024]{1,0:T(8,128)(2,1)S(1)}, u32[]{:S(2)}, u32[]{:S(2)}) collective-permute-start(bf16[256,1024]{1,0:T(8,128)(2,1)S(1)} %bitcast.168), channel_id=1, source_target_pairs={{0,8},{8,16},{16,24},{24,0},{1,9},{9,17},{17,25},{25,1},{2,10},{10... | collective-permute-start | bytes 1572872 | tf_op jit(solution)/shard_map/ppermute | solution.py:1308
  101.5 17.0 %collective-permute-start.29 = (bf16[64,1024]{1,0:T(8,128)(2,1)S(1)}, bf16[64,1024]{1,0:T(8,128)(2,1)S(1)}, u32[]{:S(2)}, u32[]{:S(2)}) collective-permute-start(bf16[64,1024]{1,0:T(8,128)(2,1)S(1)} %fusion.28.refs_8_.refs_5_), channel_id=1, source_target_pairs={{0,4},{2,6},{4,0},{6,2},{1,5},{3,7},{5,1},{7,3},{8,12},{10,14},{12... | collective-permute-start | bytes 393224 | tf_op jit(solution)/shard_map/ppermute | solution.py:1308
  105.8 17.6 %collective-permute-start.19 = (bf16[64,1024]{1,0:T(8,128)(2,1)}, bf16[64,1024]{1,0:T(8,128)(2,1)S(1)}, u32[]{:S(2)}, u32[]{:S(2)}) collective-permute-start(bf16[64,1024]{1,0:T(8,128)(2,1)} %get-tuple-element.92), channel_id=1, source_target_pairs={{0,4},{2,6},{4,0},{6,2},{1,5},{3,7},{5,1},{7,3},{8,12},{10,14},{12... | collective-permute-start | bytes 393224 | tf_op jit(solution)/shard_map/ppermute | solution.py:1312
  107.4 16.1 %collective-permute-start.20 = (bf16[64,1024]{1,0:T(8,128)(2,1)}, bf16[64,1024]{1,0:T(8,128)(2,1)S(1)}, u32[]{:S(2)}, u32[]{:S(2)}) collective-permute-start(bf16[64,1024]{1,0:T(8,128)(2,1)} %get-tuple-element.93), channel_id=1, source_target_pairs={{0,6},{2,0},{4,2},{6,4},{1,7},{3,1},{5,3},{7,5},{8,14},{10,8},{12,... | collective-permute-start | bytes 393224 | tf_op jit(solution)/shard_map/ppermute | solution.py:1312
  110.3 18.5 %collective-permute-start.30 = (bf16[64,1024]{1,0:T(8,128)(2,1)S(1)}, bf16[64,1024]{1,0:T(8,128)(2,1)S(1)}, u32[]{:S(2)}, u32[]{:S(2)}) collective-permute-start(bf16[64,1024]{1,0:T(8,128)(2,1)S(1)} %fusion.28.refs_8_.refs_5_), channel_id=1, source_target_pairs={{0,2},{2,4},{4,6},{6,0},{1,3},{3,5},{5,7},{7,1},{8,10},{10,12},{12... | collective-permute-start | bytes 393224 | tf_op jit(solution)/shard_map/ppermute | solution.py:1308
  160.7 45.4 %collective-permute-start.78 = (bf16[256,768]{1,0:T(8,128)(2,1)S(1)}, bf16[256,768]{1,0:T(8,128)(2,1)S(1)}, u32[]{:S(2)}, u32[]{:S(2)}) collective-permute-start(bf16[256,768]{1,0:T(8,128)(2,1)S(1)} %pad_maximum_fusion), channel_id=1, source_target_pairs={{0,8},{8,16},{16,24},{24,0},{1,9},{9,17},{17,25},{25,1},{2,10},{10... | collective-permute-start | bytes 1179656 | tf_op jit(solution)/shard_map/ppermute | solution.py:1312
  208.5 26.2 %collective-permute-start.53 = (f32[8,512]{1,0:T(8,128)S(1)}, f32[8,512]{1,0:T(8,128)S(1)}, u32[]{:S(2)}, u32[]{:S(2)}) collective-permute-start(f32[8,512]{1,0:T(8,128)S(1)} %add.252), channel_id=1, source_target_pairs={{0,4},{2,6},{4,0},{6,2},{1,5},{3,7},{5,1},{7,3},{8,12},{10,14},{12... | collective-permute-start | bytes 49160 | tf_op jit(solution)/shard_map/ppermute | solution.py:1308
  212.4 50.7 %collective-permute-start.81 = (bf16[64,768]{1,0:T(8,128)(2,1)S(1)}, bf16[64,768]{1,0:T(8,128)(2,1)S(1)}, u32[]{:S(2)}, u32[]{:S(2)}) collective-permute-start(bf16[64,768]{1,0:T(8,128)(2,1)S(1)} %get-tuple-element.206), channel_id=1, source_target_pairs={{0,6},{2,0},{4,2},{6,4},{1,7},{3,1},{5,3},{7,5},{8,14},{10,8},{12,... | collective-permute-start | bytes 294920 | tf_op jit(solution)/shard_map/ppermute | solution.py:1308
  215.0 48.6 %collective-permute-start.82 = (bf16[64,768]{1,0:T(8,128)(2,1)S(1)}, bf16[64,768]{1,0:T(8,128)(2,1)S(1)}, u32[]{:S(2)}, u32[]{:S(2)}) collective-permute-start(bf16[64,768]{1,0:T(8,128)(2,1)S(1)} %get-tuple-element.205), channel_id=1, source_target_pairs={{0,4},{2,6},{4,0},{6,2},{1,5},{3,7},{5,1},{7,3},{8,12},{10,14},{12... | collective-permute-start | bytes 294920 | tf_op jit(solution)/shard_map/ppermute | solution.py:1308
  223.8 39.9 %collective-permute-start.83 = (bf16[64,768]{1,0:T(8,128)(2,1)S(1)}, bf16[64,768]{1,0:T(8,128)(2,1)S(1)}, u32[]{:S(2)}, u32[]{:S(2)}) collective-permute-start(bf16[64,768]{1,0:T(8,128)(2,1)S(1)} %get-tuple-element.203), channel_id=1, source_target_pairs={{0,2},{2,4},{4,6},{6,0},{1,3},{3,5},{5,7},{7,1},{8,10},{10,12},{12... | collective-permute-start | bytes 294920 | tf_op jit(solution)/shard_map/ppermute | solution.py:1308
  225.0 40.5 %collective-permute-start.72 = (bf16[256,256]{1,0:T(8,128)(2,1)}, bf16[256,256]{1,0:T(8,128)(2,1)}, u32[]{:S(2)}, u32[]{:S(2)}) collective-permute-start(bf16[256,256]{1,0:T(8,128)(2,1)} %convolution_convert_fusion.11), channel_id=1, source_target_pairs={{0,8},{8,16},{16,24},{24,0},{1,9},{9,17},{17,25},{25,1},{2,10},{10... | collective-permute-start | bytes 393224 | tf_op jit(solution)/shard_map/ppermute | solution.py:1312
  234.7 31.9 %collective-permute-start.73 = (bf16[256,256]{1,0:T(8,128)(2,1)}, bf16[256,256]{1,0:T(8,128)(2,1)}, u32[]{:S(2)}, u32[]{:S(2)}) collective-permute-start(bf16[256,256]{1,0:T(8,128)(2,1)} %convolution_convert_fusion.10), channel_id=1, source_target_pairs={{0,16},{8,24},{16,0},{24,8},{1,17},{9,25},{17,1},{25,9},{2,18},{10... | collective-permute-start | bytes 393224 | tf_op jit(solution)/shard_map/ppermute | solution.py:1312
  263.6 33.0 %collective-permute-start.46 = (bf16[256,1024]{1,0:T(8,128)(2,1)}, bf16[256,1024]{1,0:T(8,128)(2,1)S(1)}, u32[]{:S(2)}, u32[]{:S(2)}) collective-permute-start(bf16[256,1024]{1,0:T(8,128)(2,1)} %get-tuple-element.109), channel_id=1, source_target_pairs={{0,1},{1,0},{2,3},{3,2},{4,5},{5,4},{6,7},{7,6},{8,9},{9,8},{10,11... | collective-permute-start | bytes 1572872 | tf_op jit(solution)/shard_map/ppermute | solution.py:1312
  263.7 24.4 %collective-permute-start.65 = (bf16[256,896]{1,0:T(8,128)(2,1)}, bf16[256,896]{1,0:T(8,128)(2,1)}, u32[]{:S(2)}, u32[]{:S(2)}) collective-permute-start(bf16[256,896]{1,0:T(8,128)(2,1)} %convolution_convert_fusion.2), channel_id=1, source_target_pairs={{0,8},{8,16},{16,24},{24,0},{1,9},{9,17},{17,25},{25,1},{2,10},{10... | collective-permute-start | bytes 1376264 | tf_op jit(solution)/shard_map/ppermute | solution.py:1312
  265.5 22.6 %collective-permute-start.66 = (bf16[256,896]{1,0:T(8,128)(2,1)}, bf16[256,896]{1,0:T(8,128)(2,1)}, u32[]{:S(2)}, u32[]{:S(2)}) collective-permute-start(bf16[256,896]{1,0:T(8,128)(2,1)} %convolution_convert_fusion.1), channel_id=1, source_target_pairs={{0,16},{8,24},{16,0},{24,8},{1,17},{9,25},{17,1},{25,9},{2,18},{10... | collective-permute-start | bytes 1376264 | tf_op jit(solution)/shard_map/ppermute | solution.py:1312
  266.5 21.6 %collective-permute-start.67 = (bf16[256,896]{1,0:T(8,128)(2,1)}, bf16[256,896]{1,0:T(8,128)(2,1)}, u32[]{:S(2)}, u32[]{:S(2)}) collective-permute-start(bf16[256,896]{1,0:T(8,128)(2,1)} %convolution_convert_fusion), channel_id=1, source_target_pairs={{0,24},{8,0},{16,8},{24,16},{1,25},{9,1},{17,9},{25,17},{2,26},{10... | collective-permute-start | bytes 1376264 | tf_op jit(solution)/shard_map/ppermute | solution.py:1312
  286.0 16.0 %collective-permute-start.55 = (bf16[256,1024]{1,0:T(8,128)(2,1)}, bf16[256,1024]{1,0:T(8,128)(2,1)}, u32[]{:S(2)}, u32[]{:S(2)}) collective-permute-start(bf16[256,1024]{1,0:T(8,128)(2,1)} %get-tuple-element.122), channel_id=1, source_target_pairs={{0,1},{1,0},{2,3},{3,2},{4,5},{5,4},{6,7},{7,6},{8,9},{9,8},{10,11... | collective-permute-start | bytes 1572872 | tf_op jit(solution)/shard_map/ppermute | solution.py:1312
  291.0 15.2 %collective-permute-start.68 = (bf16[64,896]{0,1:T(8,128)(2,1)}, bf16[64,896]{0,1:T(8,128)(2,1)S(1)}, u32[]{:S(2)}, u32[]{:S(2)}) collective-permute-start(bf16[64,896]{0,1:T(8,128)(2,1)} %bitcast.32), channel_id=1, source_target_pairs={{0,6},{2,0},{4,2},{6,4},{1,7},{3,1},{5,3},{7,5},{8,14},{10,8},{12,... | collective-permute-start | bytes 344072 | tf_op jit(solution)/shard_map/ppermute | solution.py:1308
  294.5 27.4 %collective-permute-start.69 = (bf16[64,896]{0,1:T(8,128)(2,1)}, bf16[64,896]{0,1:T(8,128)(2,1)S(1)}, u32[]{:S(2)}, u32[]{:S(2)}) collective-permute-start(bf16[64,896]{0,1:T(8,128)(2,1)} %bitcast.34), channel_id=1, source_target_pairs={{0,4},{2,6},{4,0},{6,2},{1,5},{3,7},{5,1},{7,3},{8,12},{10,14},{12... | collective-permute-start | bytes 344072 | tf_op jit(solution)/shard_map/ppermute | solution.py:1308
  296.6 25.4 %collective-permute-start.70 = (bf16[64,896]{0,1:T(8,128)(2,1)}, bf16[64,896]{0,1:T(8,128)(2,1)S(1)}, u32[]{:S(2)}, u32[]{:S(2)}) collective-permute-start(bf16[64,896]{0,1:T(8,128)(2,1)} %bitcast.36), channel_id=1, source_target_pairs={{0,2},{2,4},{4,6},{6,0},{1,3},{3,5},{5,7},{7,1},{8,10},{10,12},{12... | collective-permute-start | bytes 344072 | tf_op jit(solution)/shard_map/ppermute | solution.py:1308
  299.6 43.7 %collective-permute-start.47 = (bf16[64,1024]{1,0:T(8,128)(2,1)}, bf16[64,1024]{1,0:T(8,128)(2,1)S(1)}, u32[]{:S(2)}, u32[]{:S(2)}) collective-permute-start(bf16[64,1024]{1,0:T(8,128)(2,1)} %get-tuple-element.111), channel_id=1, source_target_pairs={{0,2},{2,4},{4,6},{6,0},{1,3},{3,5},{5,7},{7,1},{8,10},{10,12},{12... | collective-permute-start | bytes 393224 | tf_op jit(solution)/shard_map/ppermute | solution.py:1312
  301.9 41.4 %collective-permute-start.48 = (bf16[64,1024]{1,0:T(8,128)(2,1)}, bf16[64,1024]{1,0:T(8,128)(2,1)S(1)}, u32[]{:S(2)}, u32[]{:S(2)}) collective-permute-start(bf16[64,1024]{1,0:T(8,128)(2,1)} %get-tuple-element.112), channel_id=1, source_target_pairs={{0,4},{2,6},{4,0},{6,2},{1,5},{3,7},{5,1},{7,3},{8,12},{10,14},{12... | collective-permute-start | bytes 393224 | tf_op jit(solution)/shard_map/ppermute | solution.py:1312
  306.2 37.1 %collective-permute-start.49 = (bf16[64,1024]{1,0:T(8,128)(2,1)}, bf16[64,1024]{1,0:T(8,128)(2,1)}, u32[]{:S(2)}, u32[]{:S(2)}) collective-permute-start(bf16[64,1024]{1,0:T(8,128)(2,1)} %get-tuple-element.113), channel_id=1, source_target_pairs={{0,6},{2,0},{4,2},{6,4},{1,7},{3,1},{5,3},{7,5},{8,14},{10,8},{12,... | collective-permute-start | bytes 393224 | tf_op jit(solution)/shard_map/ppermute | solution.py:1312
  348.0 16.5 %collective-permute-start.59 = (f32[64,1024]{1,0:T(8,128)S(1)}, f32[64,1024]{1,0:T(8,128)S(1)}, u32[]{:S(2)}, u32[]{:S(2)}) collective-permute-start(f32[64,1024]{1,0:T(8,128)S(1)} %copy-done.22), channel_id=1, source_target_pairs={{0,1},{1,0},{2,3},{3,2},{4,5},{5,4},{6,7},{7,6},{8,9},{9,8},{10,11... | collective-permute-start | bytes 786440 | tf_op jit(solution)/shard_map/ppermute | solution.py:1312
  (139 other events, 1204.3 us)
